TPU v7x, 128 devices: a whole 4x4x4 slice. The times are simulated.
128 devices in a mesh: group: 32 (over x, z, y_hi), grid: 4 (over y_lo, core).
Axes of the slice: x: 4, y: 4 (y_hi: 2, y_lo: 2; y = y_hi * 2 + y_lo), z: 4, core: 2. Of those that a mesh axis runs over, the one named last changes fastest.
Arguments:
- stochastic: bfloat16 [1024, 32, 1024], P('group', 'grid'), may hold values from -6 to 6
- plane_map: int32 [32, 1024], P('group'), may hold values from 0 to 1023, each once within a row
- core_orbitals: bfloat16 [32, 512, 32, 1024], P('group', None, 'grid'), may hold values from -0.03125 to 0.03125
- potential: float32 [32, 32, 1024], P('group', 'grid'), may hold values from 0 to 0.4
Outputs:
- density: float32 [32, 32, 1024], P('group', 'grid')
- own_filtered: float32 [1024, 32, 1024], P('group', 'grid')
Inputs may be any that keep to these rules, and one draw needn't show every extreme that they name: `plane_map`: each row names every plane point once.
All inputs are finite; a program needn't handle non-finite values.
Results may differ from a plain program's by a relative error of at most 0.001.
Values may be sent and summed in bfloat16 or wider, within the bound.
No kernel may reach another device: no remote copies, remote signals or barrier semaphores. Data moves between devices by JAX's collectives and lax.ppermute only.
A program may use at most 128 MiB of HBM per device.

v0:
```python
from fractions import Fraction

import jax
import jax.numpy as jnp
from jax import lax
from jax.experimental import pallas as pl
from jax.experimental.pallas import tpu as pltpu
from jax.sharding import PartitionSpec as P


BZ = 32
KDEG = 6
BATCH = 32
NCORE = 512
SLAB = 8
PLANE = 1024
GRID = 4
HALO = KDEG
WIDE = SLAB + 2 * HALO
LANES = 128
TILES = PLANE // LANES
F32 = jnp.float32
BF16 = jnp.bfloat16


def horner_coefficients():
    cheb = [[Fraction(1)], [Fraction(0), Fraction(1)]]
    for _ in range(2, KDEG + 1):
        last, before = cheb[-1], cheb[-2]
        nxt = [Fraction(0)] + [2 * v for v in last]
        for i, v in enumerate(before):
            nxt[i] -= v
        cheb.append(nxt)
    mono = [Fraction(0)] * (KDEG + 1)
    for k, poly in enumerate(cheb):
        for i, v in enumerate(poly):
            mono[i] += v / (k + 1)
    scaled = [v / Fraction(-8) ** i for i, v in enumerate(mono)]
    top = scaled[KDEG]
    return [float(v / top) for v in scaled], float(top)


EK, TOP = horner_coefficients()

VMEM = pl.BlockSpec(memory_space=pltpu.VMEM)
ANY = pl.BlockSpec(memory_space=pl.ANY)
MIB = 1 << 20
PIECE = 32
SCALE = 500e6
CHUNKS = NCORE // PIECE
NT = (((1,), (1,)), ((), ()))


class Line:
    def __init__(self):
        self.token = None

    def call(self, kernel, out_shape, args, specs=None, scratch=(), limit=8, micros=2):
        specs = list(specs or [VMEM] * len(args))
        args = list(args)
        waits = self.token is not None
        if waits:
            args.append(self.token)
            specs.append(ANY)
        outs = tuple(out_shape) + (struct((8, LANES), F32),)

        def with_token(*refs):
            ins, rest = refs[: len(args)], refs[len(args) :]
            mine, token, extra = rest[: len(outs) - 1], rest[len(outs) - 1], rest[len(outs) :]
            kernel(*ins[: len(args) - waits], *mine, *extra)
            token[...] = jnp.zeros((8, LANES), F32)

        got = pl.pallas_call(
            with_token,
            in_specs=specs,
            out_specs=tuple(VMEM for _ in outs),
            out_shape=outs,
            scratch_shapes=list(scratch),
            compiler_params=pltpu.CompilerParams(vmem_limit_bytes=limit * MIB),
            cost_estimate=pl.CostEstimate(
                flops=int(micros * SCALE), bytes_accessed=1024, transcendentals=0
            ),
        )(*args)
        self.token = got[-1]
        return got[:-1]


def struct(shape, dtype):
    return jax.ShapeDtypeStruct(shape, dtype)


def one_hot(condition):
    return jnp.where(condition, 1.0, 0.0).astype(BF16)


def iota(shape, axis):
    return lax.broadcasted_iota(jnp.int32, shape, axis)


def dot(a, b):
    return jnp.dot(a, b, preferred_element_type=F32)


def dot_nt(a, b):
    return lax.dot_general(a, b, NT, preferred_element_type=F32)


def split(value, parts):
    out = []
    for _ in range(parts):
        out.append(value.astype(BF16))
        value = value - out[-1].astype(F32)
    return out


def row_permutation(rows, inner):
    outer = rows // inner
    out, src = iota((rows, rows), 0), iota((rows, rows), 1)
    return one_hot(src == (out % outer) * inner + out // outer)


def natural_point(q):
    tile, lane = q // LANES, q % LANES
    return (4 * (lane // 16) + tile // 2) * BZ + 2 * (lane % 16) + tile % 2


def prepare_kernel(index_ref, local_ref, order_ref, pick_ref, local_out):
    order_ref[...] = one_hot(iota((PLANE, PLANE), 1) == natural_point(iota((PLANE, PLANE), 0)))
    index = index_ref[...]
    digits = jnp.concatenate([index // 32, index % 32] + [jnp.zeros((6, PLANE), jnp.int32)], axis=0)
    rows = jnp.concatenate([digits.astype(F32)] + [p.astype(F32) for p in split(local_ref[...], 3)], axis=0)
    moved = dot_nt(rows.astype(BF16), order_ref[...])
    local_out[...] = (moved[8:16] + moved[16:24]) + moved[24:32]
    index = (moved[0:1] * 32.0 + moved[1:2]).astype(jnp.int32)
    pick_ref[...] = one_hot(iota((PLANE, PLANE), 0) == index)


def prepare(line, plane_map, local):
    square = struct((PLANE, PLANE), BF16)
    return line.call(
        prepare_kernel, (square, square, struct((SLAB, PLANE), F32)), (plane_map, local), micros=2
    )


def relayout_kernel(core_hbm, out_ref, raw, wide, columns_ref, sems):
    def fetch(i):
        return pltpu.make_async_copy(core_hbm.at[pl.ds(i * 256, 256), :], raw.at[i], sems.at[i])

    for i in range(8):
        fetch(i).start()
    src, out = iota((256, 256), 0), iota((256, 256), 1)
    for b in range(4):
        piece, low = 4 * (out // LANES) + (out // PIECE - b) % 4, out % PIECE
        columns_ref[b] = one_hot(
            src == (4 * (low // 16) + piece // 2) * BZ + 2 * (low % 16) + piece % 2
        )
    quarter = iota((PIECE, LANES), 1) // PIECE

    def permute(i, k):
        for b in range(4):
            moved = dot(raw[i, :, pl.ds(b * 256, 256)], columns_ref[b])
            wide[k, b, 0] = moved[:, :LANES]
            wide[k, b, 1] = moved[:, LANES:]

    def gather(i, k):
        at = pl.ds(pl.multiple_of(i * PIECE, PIECE), PIECE)
        for x in range(SLAB):
            rows = pl.ds(x, PIECE, stride=SLAB)
            for h in range(2):
                p = [wide[k, b, h, rows, :].astype(BF16) for b in range(4)]
                for q in range(4):
                    taken = p[3]
                    for b in range(3):
                        taken = jnp.where(quarter == (q + b) % 4, p[b], taken)
                    if q:
                        taken = pltpu.roll(taken, LANES - q * PIECE, 1)
                    out_ref[x, at, pl.ds((4 * h + q) * LANES, LANES)] = taken

    @pl.loop(0, CHUNKS // 4)
    def _(i):
        @pl.when(i < CHUNKS // 4 - 2)
        def _():
            for k in range(4):
                fetch(4 * i + 8 + k).start()

        for k in range(4):
            fetch(4 * i + k).wait()
        for k in range(5):
            if k < 4:
                permute(4 * i + k, k)
            if k > 0:
                gather(4 * i + k - 1, k - 1)


def relayout(line, core):
    return line.call(
        relayout_kernel,
        (struct((SLAB, NCORE, PLANE), BF16),),
        (core.reshape(NCORE * SLAB, PLANE),),
        specs=[pl.BlockSpec(memory_space=pltpu.HBM)],
        scratch=[
            pltpu.VMEM((CHUNKS, 256, PLANE), BF16),
            pltpu.VMEM((4, 4, 2, 256, LANES), F32),
            pltpu.VMEM((4, 256, 256), BF16),
            pltpu.SemaphoreType.DMA((CHUNKS,)),
        ],
        limit=42,
        micros=8,
    )[0]


def sums(field_of, core_ref, full_ref, half_ref):
    for x in range(SLAB):
        part = dot_nt(field_of(x), core_ref[x])
        if x == 0:
            full_ref[...] = part
        else:
            full_ref[...] += part
    half_ref[...] = full_ref[...].astype(BF16)


def map_kernel(counts, pick_ref, core_ref, *refs):
    sources, (out_ref, full_ref, half_ref) = refs[:-3], refs[-3:]
    perm = row_permutation(BATCH * SLAB, SLAB)
    for b, count in enumerate(counts):
        value = sources[0][...]
        if count == 2:
            odd = lax.axis_index("group") % 2 == 1
            value = jnp.where(odd, value, sources[1][...])
        sources = sources[count:]
        got = dot(dot(perm, value).astype(BF16), pick_ref[...]).astype(BF16)
        out_ref[:, b * BATCH : (b + 1) * BATCH, :] = got.reshape(SLAB, BATCH, PLANE)
    sums(lambda x: out_ref[x], core_ref, full_ref, half_ref)


def map_batches(line, pick, core_x, batches):
    rows = BATCH * len(batches)
    counts = tuple(len(b) for b in batches)
    flat = [a.reshape(BATCH * SLAB, PLANE) for b in batches for a in b]
    return line.call(
        lambda *refs: map_kernel(counts, *refs),
        (struct((SLAB, rows, PLANE), BF16), struct((rows, NCORE), F32), struct((rows, NCORE), BF16)),
        (pick, core_x, *flat),
        micros=2 + len(batches) // 2,
    )


def exchange(half):
    return [
        lax.ppermute(half, "grid", [(i, i ^ k) for i in range(GRID)]) for k in range(1, GRID)
    ]


def total_of(full_ref, a_ref, b_ref, c_ref):
    rest = a_ref[...].astype(F32) + b_ref[...].astype(F32) + c_ref[...].astype(F32)
    return (full_ref[...] + rest).astype(BF16)


def project_kernel(full_ref, a_ref, b_ref, c_ref, field_ref, core_ref, *refs):
    local_ref = refs[0] if len(refs) == 4 else None
    out_ref, low_ref, high_ref = refs[-3:]
    coef = total_of(full_ref, a_ref, b_ref, c_ref)
    for x in range(SLAB):
        value = field_ref[x].astype(F32) - dot(coef, core_ref[x])
        out_ref[x] = value
        short = value.astype(BF16)
        if local_ref is not None:
            parts = [p.astype(F32) for p in split(local_ref[x : x + 1], 3)]
            rest = jnp.zeros((12, PLANE), F32)
            extra = jnp.concatenate(parts + [jnp.ones((1, PLANE), F32), rest], axis=0)
            short = jnp.concatenate([short, extra.astype(BF16)], axis=0)
        if x < HALO:
            low_ref[x] = short
        if x >= SLAB - HALO:
            high_ref[x - (SLAB - HALO)] = short


def project(line, full, others, field, core_x, local):
    rows = field.shape[1]
    sent = rows + (16 if local is not None else 0)
    return line.call(
        project_kernel,
        (
            struct((SLAB, rows, PLANE), F32),
            struct((HALO, sent, PLANE), BF16),
            struct((HALO, sent, PLANE), BF16),
        ),
        (full, *others, field, core_x) + ((local,) if local is not None else ()),
        micros=2,
    )


UP = [(i, i + 1) for i in range(GRID - 1)]
DOWN = [(j, i) for i, j in UP]


def filter_kernel(ahead, *refs):
    field_ref, below_ref, above_ref = refs[:3]
    if ahead:
        local_ref, weight_ref, first_ref, flag_ref, out_ref = refs[3:8]
    else:
        weight_ref, first_ref, flag_ref, core_ref, other_ref, out_ref, full_ref, half_ref = refs[3:11]
    below, above, even, odd = refs[-4:]
    rows = field_ref.shape[1]
    if ahead:
        weight_ref[HALO : HALO + SLAB] = 8.0 * local_ref[...] - 2.0
        for k, ref in enumerate((below_ref, above_ref)):
            for x in range(HALO):
                extra = ref[x, rows : rows + 16, :].astype(F32)
                near = (extra[0:1] + extra[1:2]) + extra[2:3]
                place = x if k == 0 else HALO + SLAB + x
                weight_ref[place : place + 1] = 8.0 * near - 2.0
                if x == 0:
                    flag_ref[k] = jnp.broadcast_to(extra[3:4, :LANES], (8, LANES))
        first_ref[...] = weight_ref[...] - EK[KDEG - 1]
    lane = iota((8, LANES), 1)
    head, tail = lane < 16, lane >= LANES - 16
    first_z, last_z = lane % 16 == 0, lane % 16 == 15
    low_flag, high_flag = flag_ref[0], flag_ref[1]

    def rolled(mask, value, by):
        return pltpu.roll(jnp.where(mask, 0.0, value), by % LANES, 1)

    def sweep(local, at):
        def begin(x, lanes):
            if x < HALO:
                return below[x, local, lanes]
            if x >= HALO + SLAB:
                return above[x - HALO - SLAB, local, lanes]
            return field_ref[x - HALO, at, lanes]

        def tiles(source, x):
            every = [pl.ds(j * LANES, LANES) for j in range(TILES)]
            if source is None:
                return [begin(x, lanes) for lanes in every]
            return [source[x, :, lanes] for lanes in every]

        source = None
        for k in range(1, KDEG + 1):
            target = even if k % 2 == 0 else odd
            first, last = k, WIDE - k
            here, after = tiles(source, first - 1), tiles(source, first)
            for x in range(first, last):
                before, here = here, after
                after = tiles(source, x + 1)
                up = [rolled(head, here[j], -16) for j in range(2)]
                down = [rolled(tail, here[j], 16) for j in range(6, 8)]
                for j in range(TILES):
                    lanes = pl.ds(j * LANES, LANES)
                    c = here[j]
                    above_y = here[j + 2] if j < 6 else up[j - 6]
                    below_y = here[j - 2] if j > 1 else down[j]
                    mate = here[j ^ 1]
                    z = mate + (rolled(first_z, mate, -1) if j % 2 else rolled(last_z, mate, 1))
                    around = (before[j] + after[j]) + (above_y + below_y) + z
                    w_ref = first_ref if k == 1 else weight_ref
                    w = jnp.broadcast_to(w_ref[pl.ds(x, 1), lanes], (8, LANES))
                    value = around - w * c
                    if k > 1:
                        value = value + EK[KDEG - k] * begin(x, lanes)
                    if x == HALO - 1:
                        value = value * low_flag
                    elif x == HALO + SLAB:
                        value = value * high_flag
                    if k == KDEG:
                        out_ref[x - HALO, at, lanes] = value * TOP
                    else:
                        target[x, :, lanes] = value
            source = target

    @pl.loop(0, rows // 16)
    def _(i):
        both = pl.ds(pl.multiple_of(i * 16, 16), 16)
        below[...] = below_ref[:, both, :].astype(F32)
        above[...] = above_ref[:, both, :].astype(F32)

        @pl.loop(0, 2)
        def _(k):
            sweep(
                pl.ds(pl.multiple_of(k * 8, 8), 8),
                pl.ds(pl.multiple_of(i * 16 + k * 8, 8), 8),
            )

    if not ahead:

        def both_of(x):
            return jnp.concatenate([other_ref[x].astype(BF16), out_ref[x].astype(BF16)], axis=0)

        sums(both_of, core_ref, full_ref, half_ref)


def filter_scratch():
    halo, whole = pltpu.VMEM((HALO, 16, PLANE), F32), pltpu.VMEM((WIDE, 8, PLANE), F32)
    return [halo, halo, whole, whole]


def filter_ahead(line, field, below, above, local):
    rows = field.shape[1]
    wide = struct((WIDE, PLANE), F32)
    got = line.call(
        lambda *refs: filter_kernel(True, *refs),
        (wide, wide, struct((2, 8, LANES), F32), struct((SLAB, rows, PLANE), F32)),
        (field, below, above, local),
        scratch=filter_scratch(),
        micros=7,
    )
    return got[:3], got[3]


def filter_rest(line, field, below, above, weight, core_x, ahead):
    rows = field.shape[1]
    total = rows + ahead.shape[1]
    return line.call(
        lambda *refs: filter_kernel(False, *refs),
        (struct((SLAB, rows, PLANE), F32), struct((total, NCORE), F32), struct((total, NCORE), BF16)),
        (field, below, above, *weight, core_x, ahead),
        scratch=filter_scratch(),
        micros=14,
    )


def reorder(value, order_ref):
    parts = split(value, 2)
    return dot(parts[0], order_ref[...]) + dot(parts[1], order_ref[...])


def clean_kernel(full_ref, a_ref, b_ref, c_ref, ahead_ref, rest_ref, mapped_ref, mapped_rest_ref, core_ref, order_ref, own_ref, density_ref, own, rows):
    coef = total_of(full_ref, a_ref, b_ref, c_ref)
    for x in range(SLAB):
        taken = dot(coef, core_ref[x])
        ahead = ahead_ref[x] - taken[: ahead_ref.shape[1]]
        rest = rest_ref[x] - taken[ahead_ref.shape[1] :]
        own[x * BATCH : (x + 1) * BATCH] = ahead[:BATCH]
        weighted = jnp.sum(mapped_ref[x].astype(F32) * ahead, axis=0, keepdims=True)
        weighted += jnp.sum(mapped_rest_ref[x].astype(F32) * rest, axis=0, keepdims=True)
        rows[x : x + 1] = weighted / (3.0 * BATCH)
    back = row_permutation(BATCH * SLAB, BATCH)
    total = None
    for part in split(own[...], 2):
        moved = dot(dot(back, part).astype(BF16), order_ref[...])
        total = moved if total is None else total + moved
    own_ref[...] = total
    density_ref[...] = reorder(rows[...], order_ref)


def clean(line, full, others, ahead, rest, mapped, mapped_rest, core_x, order):
    small, own = struct((SLAB, PLANE), F32), struct((SLAB * BATCH, PLANE), F32)
    return line.call(
        clean_kernel,
        (own, small),
        (full, *others, ahead, rest, mapped, mapped_rest, core_x, order),
        scratch=[pltpu.VMEM(own.shape, F32), pltpu.VMEM(small.shape, F32)],
        limit=12,
        micros=4,
    )


def permute_groups(array, pairs):
    return lax.ppermute(array, "group", pairs)


def body(stochastic, plane_map, core_orbitals, potential):
    groups = lax.axis_size("group")
    mate = permute_groups(stochastic, [(i, i ^ 1) for i in range(groups)])
    third = permute_groups(stochastic, [(i, (i + 2) % groups) for i in range(groups)])

    line = Line()
    core_x = relayout(line, core_orbitals[0])
    order, pick, local = prepare(line, plane_map, potential[0])

    mate, line.token = lax.optimization_barrier((mate, line.token))
    second = permute_groups(mate, [(i, (i + 2) % groups) for i in range(0, groups, 2)])
    mapped, full, half = map_batches(line, pick, core_x, [(stochastic,), (third,)])
    others = exchange(half)
    field, low, high = project(line, full, others, mapped, core_x, local)
    below = lax.ppermute(high, "grid", UP)
    above = lax.ppermute(low, "grid", DOWN)

    mapped_rest, full, half = map_batches(line, pick, core_x, [(mate, second)])
    others = exchange(half)
    rest, low, high = project(line, full, others, mapped_rest, core_x, None)
    below_rest, above_rest = lax.ppermute(high, "grid", UP), lax.ppermute(low, "grid", DOWN)

    weight, ahead = filter_ahead(line, field, below, above, local)
    rest, full, half = filter_rest(line, rest, below_rest, above_rest, weight, core_x, ahead)
    own, density = clean(
        line, full, exchange(half), ahead, rest, mapped, mapped_rest, core_x, order
    )
    return density[None], own.reshape(BATCH, SLAB, PLANE)


def solution(mesh):
    return jax.shard_map(
        body,
        mesh=mesh,
        in_specs=(
            P("group", "grid", None),
            P("group", None),
            P("group", None, "grid", None),
            P("group", "grid", None),
        ),
        out_specs=(P("group", "grid", None), P("group", "grid", None)),
        check_vma=False,
    )
```

profile of v0, /device:TPU:0, one launch (start us, length us, event | category | flops | bytes accessed | tf_op | source)
XLA Modules:
  0.0 100.5 jit_solution(13243671233946669258)
XLA Ops:
  0.6 3.4 %collective-permute-start = (bf16[32,8,1024]{2,1,0:T(8,128)(2,1)}, bf16[32,8,1024]{2,1,0:T(8,128)(2,1)S(1)}, u32[]{:S(2)}, u32[]{:S(2)}) collective-permute-start(bf16[32,8,1024]{2,1,0:T(8,128)(2,1)} %param.4), channel_id=1, source_target_pairs={{0,4},{4,0},{8,12},{12,8},{16,20},{20,16},{24,28},{28,24},{32,36},... | collective-permute-start | bytes 1572872 | tf_op jit(solution)/shard_map/ppermute | solution.py:459
  4.0 1.9 %collective-permute-start.2 = (bf16[32,8,1024]{2,1,0:T(8,128)(2,1)}, bf16[32,8,1024]{2,1,0:T(8,128)(2,1)S(1)}, u32[]{:S(2)}, u32[]{:S(2)}) collective-permute-start(bf16[32,8,1024]{2,1,0:T(8,128)(2,1)} %param.4), channel_id=1, source_target_pairs={{0,8},{4,12},{8,16},{12,20},{16,24},{20,28},{24,32},{28,36},{32,40... | collective-permute-start | bytes 1572872 | tf_op jit(solution)/shard_map/ppermute | solution.py:459
  5.9 0.0 copy-start.1
  5.9 0.0 copy-start.2
  5.9 7.2 %shard_map.59 = (bf16[8,512,1024]{2,1,0:T(8,128)(2,1)S(1)}, f32[8,128]{1,0:T(8,128)S(1)}) custom-call(bf16[4096,1024]{1,0:T(8,128)(2,1)} %bitcast.13), custom_call_target="tpu_custom_call" | custom-call | flops 4000000000 | bytes 1024 | tf_op jit(solution)/shard_map/pallas_call | solution.py:73
  13.1 0.0 copy-start
  13.2 0.0 copy-done.1
  13.2 0.0 copy-done.2
  13.2 1.8 %shard_map.60 = (bf16[1024,1024]{1,0:T(8,128)(2,1)S(1)}, bf16[1024,1024]{1,0:T(8,128)(2,1)S(1)}, f32[8,1024]{1,0:T(8,128)S(1)}, f32[8,128]{1,0:T(8,128)S(1)}) custom-call(s32[1,1024]{1,0:T(1,128)S(1)} %copy-done.2, f32[8,1024]{1,0:T(8,128)S(1)} %bitcast.12, f32[8,128]{1,0:T(8,128)S(1)} %get-tuple-element.37.refs_2_), custom_call_target="tpu_custom_call" | custom-call | flops 1000000000 | bytes 1024 | tf_op jit(solution)/shard_map/pallas_call | solution.py:73
  15.0 1.1 %collective-permute-done = bf16[32,8,1024]{2,1,0:T(8,128)(2,1)S(1)} collective-permute-done((bf16[32,8,1024]{2,1,0:T(8,128)(2,1)}, bf16[32,8,1024]{2,1,0:T(8,128)(2,1)S(1)}, u32[]{:S(2)}, u32[]{:S(2)}) %collective-permute-start) | collective-permute-done | bytes 524320 | tf_op jit(solution)/shard_map/ppermute | solution.py:459
  16.2 6.0 %collective-permute-done.2 = bf16[32,8,1024]{2,1,0:T(8,128)(2,1)S(1)} collective-permute-done((bf16[32,8,1024]{2,1,0:T(8,128)(2,1)}, bf16[32,8,1024]{2,1,0:T(8,128)(2,1)S(1)}, u32[]{:S(2)}, u32[]{:S(2)}) %collective-permute-start.2) | collective-permute-done | bytes 524320 | tf_op jit(solution)/shard_map/ppermute | solution.py:459
  22.1 0.0 copy-done
  22.1 4.0 %shard_map.61 = (bf16[8,64,1024]{2,1,0:T(8,128)(2,1)S(1)}, f32[64,512]{1,0:T(8,128)S(1)}, bf16[64,512]{1,0:T(8,128)(2,1)S(1)}, f32[8,128]{1,0:T(8,128)S(1)}) custom-call(bf16[1024,1024]{1,0:T(8,128)(2,1)S(1)} %get-tuple-element.38.refs_0_, bf16[8,512,1024]{2,1,0:T(8,128)(2,1)S(1)} %get-tuple-element.39.refs_1_.refs_5_.refs_6_.refs_8_, ...), custom_call_target="tpu_custom_call" | custom-call | flops 1500000000 | bytes 1024 | tf_op jit(solution)/shard_map/pallas_call | solution.py:73
  26.2 0.1 collective-permute-start.5
  26.3 0.8 collective-permute-start.4
  27.0 1.1 %collective-permute-start.3 = (bf16[64,512]{1,0:T(8,128)(2,1)S(1)}, bf16[64,512]{1,0:T(8,128)(2,1)S(1)}, u32[]{:S(2)}, u32[]{:S(2)}) collective-permute-start(bf16[64,512]{1,0:T(8,128)(2,1)S(1)} %get-tuple-element.44), channel_id=1, source_target_pairs={{0,1},{1,0},{2,3},{3,2},{4,5},{5,4},{6,7},{7,6},{8,9},{9,8},{10,11... | collective-permute-start | bytes 196616 | tf_op jit(solution)/shard_map/ppermute | solution.py:250
  28.1 1.9 %collective-permute-done.5.refs_3_ = bf16[64,512]{1,0:T(8,128)(2,1)S(1)} collective-permute-done((bf16[64,512]{1,0:T(8,128)(2,1)S(1)}, bf16[64,512]{1,0:T(8,128)(2,1)S(1)}, u32[]{:S(2)}, u32[]{:S(2)}) %collective-permute-start.5) | collective-permute-done | bytes 65568 | tf_op jit(solution)/shard_map/ppermute | solution.py:250
  30.0 1.3 %collective-permute-done.4.refs_2_ = bf16[64,512]{1,0:T(8,128)(2,1)S(1)} collective-permute-done((bf16[64,512]{1,0:T(8,128)(2,1)S(1)}, bf16[64,512]{1,0:T(8,128)(2,1)S(1)}, u32[]{:S(2)}, u32[]{:S(2)}) %collective-permute-start.4) | collective-permute-done | bytes 65568 | tf_op jit(solution)/shard_map/ppermute | solution.py:250
  31.3 0.0 collective-permute-done.3.refs_1_
  31.3 1.6 %shard_map.62 = (f32[8,64,1024]{2,1,0:T(8,128)S(1)}, bf16[6,80,1024]{2,1,0:T(8,128)(2,1)S(1)}, bf16[6,80,1024]{2,1,0:T(8,128)(2,1)S(1)}, f32[8,128]{1,0:T(8,128)S(1)}) custom-call(f32[64,512]{1,0:T(8,128)S(1)} %get-tuple-element.43.refs_0_, bf16[64,512]{1,0:T(8,128)(2,1)S(1)} %collective-permute-done.3.refs_1_, ...), custom_call_target="tpu_custom_call" | custom-call | flops 1000000000 | bytes 1024 | tf_op jit(solution)/shard_map/pallas_call | solution.py:73
  32.9 2.1 %collective-permute-start.11 = (bf16[6,80,1024]{2,1,0:T(8,128)(2,1)S(1)}, bf16[6,80,1024]{2,1,0:T(8,128)(2,1)S(1)}, u32[]{:S(2)}, u32[]{:S(2)}) collective-permute-start(bf16[6,80,1024]{2,1,0:T(8,128)(2,1)S(1)} %get-tuple-element.57), channel_id=1, source_target_pairs={{0,1},{1,2},{2,3},{4,5},{5,6},{6,7},{8,9},{9,10},{10,11},{12,13},{... | collective-permute-start | bytes 2949128 | tf_op jit(solution)/shard_map/ppermute | solution.py:476
  35.0 1.3 %collective-permute-start.12 = (bf16[6,80,1024]{2,1,0:T(8,128)(2,1)S(1)}, bf16[6,80,1024]{2,1,0:T(8,128)(2,1)S(1)}, u32[]{:S(2)}, u32[]{:S(2)}) collective-permute-start(bf16[6,80,1024]{2,1,0:T(8,128)(2,1)S(1)} %get-tuple-element.58), channel_id=1, source_target_pairs={{1,0},{2,1},{3,2},{5,4},{6,5},{7,6},{9,8},{10,9},{11,10},{13,12},{... | collective-permute-start | bytes 2949128 | tf_op jit(solution)/shard_map/ppermute | solution.py:477
  36.3 1.9 %collective-permute-start.1 = (bf16[32,8,1024]{2,1,0:T(8,128)(2,1)S(1)}, bf16[32,8,1024]{2,1,0:T(8,128)(2,1)S(1)}, u32[]{:S(2)}, u32[]{:S(2)}) collective-permute-start(bf16[32,8,1024]{2,1,0:T(8,128)(2,1)S(1)} %collective-permute-done), channel_id=1, source_target_pairs={{0,8},{8,16},{16,24},{24,32},{32,40},{40,48},{48,56},{56,64},{64,7... | collective-permute-start | bytes 1572872 | tf_op jit(solution)/shard_map/ppermute | solution.py:459
  38.2 17.3 %collective-permute-done.1 = bf16[32,8,1024]{2,1,0:T(8,128)(2,1)S(1)} collective-permute-done((bf16[32,8,1024]{2,1,0:T(8,128)(2,1)S(1)}, bf16[32,8,1024]{2,1,0:T(8,128)(2,1)S(1)}, u32[]{:S(2)}, u32[]{:S(2)}) %collective-permute-start.1) | collective-permute-done | bytes 524320 | tf_op jit(solution)/shard_map/ppermute | solution.py:459
  55.5 3.2 %shard_map.63 = (bf16[8,32,1024]{2,1,0:T(8,128)(2,1)S(1)}, f32[32,512]{1,0:T(8,128)S(1)}, bf16[32,512]{1,0:T(8,128)(2,1)S(1)}, f32[8,128]{1,0:T(8,128)S(1)}) custom-call(bf16[1024,1024]{1,0:T(8,128)(2,1)S(1)} %get-tuple-element.38.refs_0_, bf16[8,512,1024]{2,1,0:T(8,128)(2,1)S(1)} %get-tuple-element.39.refs_1_.refs_5_.refs_6_.refs_8_, ...), custom_call_target="tpu_custom_call" | custom-call | flops 1000000000 | bytes 1024 | tf_op jit(solution)/shard_map/pallas_call | solution.py:73
  58.7 0.0 collective-permute-start.8
  58.8 2.3 %collective-permute-start.7 = (bf16[32,512]{1,0:T(8,128)(2,1)S(1)}, bf16[32,512]{1,0:T(8,128)(2,1)S(1)}, u32[]{:S(2)}, u32[]{:S(2)}) collective-permute-start(bf16[32,512]{1,0:T(8,128)(2,1)S(1)} %get-tuple-element.50), channel_id=1, source_target_pairs={{0,2},{1,3},{2,0},{3,1},{4,6},{5,7},{6,4},{7,5},{8,10},{9,11},{10,... | collective-permute-start | bytes 98312 | tf_op jit(solution)/shard_map/ppermute | solution.py:250
  61.1 0.0 collective-permute-start.6
  61.1 1.0 %collective-permute-done.8.refs_3_ = bf16[32,512]{1,0:T(8,128)(2,1)S(1)} collective-permute-done((bf16[32,512]{1,0:T(8,128)(2,1)S(1)}, bf16[32,512]{1,0:T(8,128)(2,1)S(1)}, u32[]{:S(2)}, u32[]{:S(2)}) %collective-permute-start.8) | collective-permute-done | bytes 32800 | tf_op jit(solution)/shard_map/ppermute | solution.py:250
  62.1 1.2 %collective-permute-done.7.refs_2_ = bf16[32,512]{1,0:T(8,128)(2,1)S(1)} collective-permute-done((bf16[32,512]{1,0:T(8,128)(2,1)S(1)}, bf16[32,512]{1,0:T(8,128)(2,1)S(1)}, u32[]{:S(2)}, u32[]{:S(2)}) %collective-permute-start.7) | collective-permute-done | bytes 32800 | tf_op jit(solution)/shard_map/ppermute | solution.py:250
  63.3 0.0 collective-permute-done.6.refs_1_
  63.3 1.5 %shard_map.64 = (f32[8,32,1024]{2,1,0:T(8,128)S(1)}, bf16[6,32,1024]{2,1,0:T(8,128)(2,1)S(1)}, bf16[6,32,1024]{2,1,0:T(8,128)(2,1)S(1)}, f32[8,128]{1,0:T(8,128)S(1)}) custom-call(f32[32,512]{1,0:T(8,128)S(1)} %get-tuple-element.49.refs_0_, bf16[32,512]{1,0:T(8,128)(2,1)S(1)} %collective-permute-done.6.refs_1_, ...), custom_call_target="tpu_custom_call" | custom-call | flops 1000000000 | bytes 1024 | tf_op jit(solution)/shard_map/pallas_call | solution.py:73
  64.9 2.5 %collective-permute-start.9 = (bf16[6,32,1024]{2,1,0:T(8,128)(2,1)S(1)}, bf16[6,32,1024]{2,1,0:T(8,128)(2,1)S(1)}, u32[]{:S(2)}, u32[]{:S(2)}) collective-permute-start(bf16[6,32,1024]{2,1,0:T(8,128)(2,1)S(1)} %get-tuple-element.54), channel_id=1, source_target_pairs={{0,1},{1,2},{2,3},{4,5},{5,6},{6,7},{8,9},{9,10},{10,11},{12,13},{... | collective-permute-start | bytes 1179656 | tf_op jit(solution)/shard_map/ppermute | solution.py:482
  67.4 1.3 %collective-permute-start.10 = (bf16[6,32,1024]{2,1,0:T(8,128)(2,1)S(1)}, bf16[6,32,1024]{2,1,0:T(8,128)(2,1)S(1)}, u32[]{:S(2)}, u32[]{:S(2)}) collective-permute-start(bf16[6,32,1024]{2,1,0:T(8,128)(2,1)S(1)} %get-tuple-element.55), channel_id=1, source_target_pairs={{1,0},{2,1},{3,2},{5,4},{6,5},{7,6},{9,8},{10,9},{11,10},{13,12},{... | collective-permute-start | bytes 1179656 | tf_op jit(solution)/shard_map/ppermute | solution.py:482
  68.7 0.0 collective-permute-done.11.refs_1_
  68.7 0.0 collective-permute-done.12.refs_2_
  68.7 11.0 %shard_map.65 = (f32[20,1024]{1,0:T(8,128)S(1)}, f32[20,1024]{1,0:T(8,128)S(1)}, f32[2,8,128]{2,1,0:T(8,128)S(1)}, f32[8,64,1024]{2,1,0:T(8,128)S(1)}, f32[8,128]{1,0:T(8,128)S(1)}) custom-call(f32[8,64,1024]{2,1,0:T(8,128)S(1)} %get-tuple-element.56.refs_0_, bf16[6,80,1024]{2,1,0:T(8,128)(2,1)S(1)} %collective-permute-done.11.refs_1_, ...), custom_call_target="tpu_custom_call" | custom-call | flops 3500000000 | bytes 1024 | tf_op jit(solution)/shard_map/pallas_call | solution.py:73
  79.7 0.0 collective-permute-done.9.refs_1_
  79.7 0.0 collective-permute-done.10.refs_2_
  79.7 8.4 %shard_map.66 = (f32[8,32,1024]{2,1,0:T(8,128)S(1)}, f32[96,512]{1,0:T(8,128)S(1)}, bf16[96,512]{1,0:T(8,128)(2,1)S(1)}, f32[8,128]{1,0:T(8,128)S(1)}) custom-call(f32[8,32,1024]{2,1,0:T(8,128)S(1)} %get-tuple-element.53.refs_0_, bf16[6,32,1024]{2,1,0:T(8,128)(2,1)S(1)} %collective-permute-done.9.refs_1_, ...), custom_call_target="tpu_custom_call" | custom-call | flops 7000000000 | bytes 1024 | tf_op jit(solution)/shard_map/pallas_call | solution.py:73
  88.1 2.0 %collective-permute-start.15 = (bf16[96,512]{1,0:T(8,128)(2,1)S(1)}, bf16[96,512]{1,0:T(8,128)(2,1)S(1)}, u32[]{:S(2)}, u32[]{:S(2)}) collective-permute-start(bf16[96,512]{1,0:T(8,128)(2,1)S(1)} %get-tuple-element.66), channel_id=1, source_target_pairs={{0,3},{1,2},{2,1},{3,0},{4,7},{5,6},{6,5},{7,4},{8,11},{9,10},{10,... | collective-permute-start | bytes 294920 | tf_op jit(solution)/shard_map/ppermute | solution.py:250
  90.0 1.7 %collective-permute-start.14 = (bf16[96,512]{1,0:T(8,128)(2,1)S(1)}, bf16[96,512]{1,0:T(8,128)(2,1)S(1)}, u32[]{:S(2)}, u32[]{:S(2)}) collective-permute-start(bf16[96,512]{1,0:T(8,128)(2,1)S(1)} %get-tuple-element.66), channel_id=1, source_target_pairs={{0,2},{1,3},{2,0},{3,1},{4,6},{5,7},{6,4},{7,5},{8,10},{9,11},{10,... | collective-permute-start | bytes 294920 | tf_op jit(solution)/shard_map/ppermute | solution.py:250
  91.7 0.0 collective-permute-start.13
  91.8 0.6 collective-permute-done.15.refs_3_
  92.4 3.9 %collective-permute-done.14.refs_2_ = bf16[96,512]{1,0:T(8,128)(2,1)S(1)} collective-permute-done((bf16[96,512]{1,0:T(8,128)(2,1)S(1)}, bf16[96,512]{1,0:T(8,128)(2,1)S(1)}, u32[]{:S(2)}, u32[]{:S(2)}) %collective-permute-start.14) | collective-permute-done | bytes 98336 | tf_op jit(solution)/shard_map/ppermute | solution.py:250
  96.2 0.0 collective-permute-done.13.refs_1_
  96.3 4.3 %shard_map.67 = (f32[256,1024]{1,0:T(8,128)}, f32[8,1024]{1,0:T(8,128)}, f32[8,128]{1,0:T(8,128)}) custom-call(f32[96,512]{1,0:T(8,128)S(1)} %get-tuple-element.65.refs_0_, bf16[96,512]{1,0:T(8,128)(2,1)S(1)} %collective-permute-done.13.refs_1_, bf16[96,512]{1,0:T(8,128)(2,1)S(1)} %collective-permute-done.14.refs_2_, ...), custom_call_target="tpu_custom_call" | custom-call | flops 2000000000 | bytes 1024 | tf_op jit(solution)/shard_map/pallas_call | solution.py:73
Async XLA Ops:
  0.6 15.5 %collective-permute-start = (bf16[32,8,1024]{2,1,0:T(8,128)(2,1)}, bf16[32,8,1024]{2,1,0:T(8,128)(2,1)S(1)}, u32[]{:S(2)}, u32[]{:S(2)}) collective-permute-start(bf16[32,8,1024]{2,1,0:T(8,128)(2,1)} %param.4), channel_id=1, source_target_pairs={{0,4},{4,0},{8,12},{12,8},{16,20},{20,16},{24,28},{28,24},{32,36},... | collective-permute-start | bytes 1572872 | tf_op jit(solution)/shard_map/ppermute | solution.py:459
  4.0 18.1 %collective-permute-start.2 = (bf16[32,8,1024]{2,1,0:T(8,128)(2,1)}, bf16[32,8,1024]{2,1,0:T(8,128)(2,1)S(1)}, u32[]{:S(2)}, u32[]{:S(2)}) collective-permute-start(bf16[32,8,1024]{2,1,0:T(8,128)(2,1)} %param.4), channel_id=1, source_target_pairs={{0,8},{4,12},{8,16},{12,20},{16,24},{20,28},{24,32},{28,36},{32,40... | collective-permute-start | bytes 1572872 | tf_op jit(solution)/shard_map/ppermute | solution.py:459
  5.9 7.2 %copy-start.1 = (f32[1,8,1024]{2,1,0:T(8,128)S(1)}, f32[1,8,1024]{2,1,0:T(8,128)}, u32[]{:S(2)}) copy-start(f32[1,8,1024]{2,1,0:T(8,128)} %param.7) | copy-start | bytes 98308
  5.9 7.2 %copy-start.2 = (s32[1,1024]{1,0:T(1,128)S(1)}, s32[1,1024]{1,0:T(1,128)}, u32[]{:S(2)}) copy-start(s32[1,1024]{1,0:T(1,128)} %refs_0_.1) | copy-start | bytes 12292
  13.1 9.0 %copy-start = (bf16[32,8,1024]{2,1,0:T(8,128)(2,1)S(1)}, bf16[32,8,1024]{2,1,0:T(8,128)(2,1)}, u32[]{:S(2)}) copy-start(bf16[32,8,1024]{2,1,0:T(8,128)(2,1)} %param.4) | copy-start | bytes 1572868
  26.2 3.8 %collective-permute-start.5 = (bf16[64,512]{1,0:T(8,128)(2,1)S(1)}, bf16[64,512]{1,0:T(8,128)(2,1)S(1)}, u32[]{:S(2)}, u32[]{:S(2)}) collective-permute-start(bf16[64,512]{1,0:T(8,128)(2,1)S(1)} %get-tuple-element.44), channel_id=1, source_target_pairs={{0,3},{1,2},{2,1},{3,0},{4,7},{5,6},{6,5},{7,4},{8,11},{9,10},{10,... | collective-permute-start | bytes 196616 | tf_op jit(solution)/shard_map/ppermute | solution.py:250
  26.3 5.0 %collective-permute-start.4 = (bf16[64,512]{1,0:T(8,128)(2,1)S(1)}, bf16[64,512]{1,0:T(8,128)(2,1)S(1)}, u32[]{:S(2)}, u32[]{:S(2)}) collective-permute-start(bf16[64,512]{1,0:T(8,128)(2,1)S(1)} %get-tuple-element.44), channel_id=1, source_target_pairs={{0,2},{1,3},{2,0},{3,1},{4,6},{5,7},{6,4},{7,5},{8,10},{9,11},{10,... | collective-permute-start | bytes 196616 | tf_op jit(solution)/shard_map/ppermute | solution.py:250
  27.0 4.3 %collective-permute-start.3 = (bf16[64,512]{1,0:T(8,128)(2,1)S(1)}, bf16[64,512]{1,0:T(8,128)(2,1)S(1)}, u32[]{:S(2)}, u32[]{:S(2)}) collective-permute-start(bf16[64,512]{1,0:T(8,128)(2,1)S(1)} %get-tuple-element.44), channel_id=1, source_target_pairs={{0,1},{1,0},{2,3},{3,2},{4,5},{5,4},{6,7},{7,6},{8,9},{9,8},{10,11... | collective-permute-start | bytes 196616 | tf_op jit(solution)/shard_map/ppermute | solution.py:250
  32.9 35.7 %collective-permute-start.11 = (bf16[6,80,1024]{2,1,0:T(8,128)(2,1)S(1)}, bf16[6,80,1024]{2,1,0:T(8,128)(2,1)S(1)}, u32[]{:S(2)}, u32[]{:S(2)}) collective-permute-start(bf16[6,80,1024]{2,1,0:T(8,128)(2,1)S(1)} %get-tuple-element.57), channel_id=1, source_target_pairs={{0,1},{1,2},{2,3},{4,5},{5,6},{6,7},{8,9},{9,10},{10,11},{12,13},{... | collective-permute-start | bytes 2949128 | tf_op jit(solution)/shard_map/ppermute | solution.py:476
  35.0 33.7 %collective-permute-start.12 = (bf16[6,80,1024]{2,1,0:T(8,128)(2,1)S(1)}, bf16[6,80,1024]{2,1,0:T(8,128)(2,1)S(1)}, u32[]{:S(2)}, u32[]{:S(2)}) collective-permute-start(bf16[6,80,1024]{2,1,0:T(8,128)(2,1)S(1)} %get-tuple-element.58), channel_id=1, source_target_pairs={{1,0},{2,1},{3,2},{5,4},{6,5},{7,6},{9,8},{10,9},{11,10},{13,12},{... | collective-permute-start | bytes 2949128 | tf_op jit(solution)/shard_map/ppermute | solution.py:477
  36.3 19.2 %collective-permute-start.1 = (bf16[32,8,1024]{2,1,0:T(8,128)(2,1)S(1)}, bf16[32,8,1024]{2,1,0:T(8,128)(2,1)S(1)}, u32[]{:S(2)}, u32[]{:S(2)}) collective-permute-start(bf16[32,8,1024]{2,1,0:T(8,128)(2,1)S(1)} %collective-permute-done), channel_id=1, source_target_pairs={{0,8},{8,16},{16,24},{24,32},{32,40},{40,48},{48,56},{56,64},{64,7... | collective-permute-start | bytes 1572872 | tf_op jit(solution)/shard_map/ppermute | solution.py:459
  58.7 3.4 %collective-permute-start.8 = (bf16[32,512]{1,0:T(8,128)(2,1)S(1)}, bf16[32,512]{1,0:T(8,128)(2,1)S(1)}, u32[]{:S(2)}, u32[]{:S(2)}) collective-permute-start(bf16[32,512]{1,0:T(8,128)(2,1)S(1)} %get-tuple-element.50), channel_id=1, source_target_pairs={{0,3},{1,2},{2,1},{3,0},{4,7},{5,6},{6,5},{7,4},{8,11},{9,10},{10,... | collective-permute-start | bytes 98312 | tf_op jit(solution)/shard_map/ppermute | solution.py:250
  58.8 4.5 %collective-permute-start.7 = (bf16[32,512]{1,0:T(8,128)(2,1)S(1)}, bf16[32,512]{1,0:T(8,128)(2,1)S(1)}, u32[]{:S(2)}, u32[]{:S(2)}) collective-permute-start(bf16[32,512]{1,0:T(8,128)(2,1)S(1)} %get-tuple-element.50), channel_id=1, source_target_pairs={{0,2},{1,3},{2,0},{3,1},{4,6},{5,7},{6,4},{7,5},{8,10},{9,11},{10,... | collective-permute-start | bytes 98312 | tf_op jit(solution)/shard_map/ppermute | solution.py:250
  61.1 2.2 %collective-permute-start.6 = (bf16[32,512]{1,0:T(8,128)(2,1)S(1)}, bf16[32,512]{1,0:T(8,128)(2,1)S(1)}, u32[]{:S(2)}, u32[]{:S(2)}) collective-permute-start(bf16[32,512]{1,0:T(8,128)(2,1)S(1)} %get-tuple-element.50), channel_id=1, source_target_pairs={{0,1},{1,0},{2,3},{3,2},{4,5},{5,4},{6,7},{7,6},{8,9},{9,8},{10,11... | collective-permute-start | bytes 98312 | tf_op jit(solution)/shard_map/ppermute | solution.py:250
  64.9 14.8 %collective-permute-start.9 = (bf16[6,32,1024]{2,1,0:T(8,128)(2,1)S(1)}, bf16[6,32,1024]{2,1,0:T(8,128)(2,1)S(1)}, u32[]{:S(2)}, u32[]{:S(2)}) collective-permute-start(bf16[6,32,1024]{2,1,0:T(8,128)(2,1)S(1)} %get-tuple-element.54), channel_id=1, source_target_pairs={{0,1},{1,2},{2,3},{4,5},{5,6},{6,7},{8,9},{9,10},{10,11},{12,13},{... | collective-permute-start | bytes 1179656 | tf_op jit(solution)/shard_map/ppermute | solution.py:482
  67.4 12.3 %collective-permute-start.10 = (bf16[6,32,1024]{2,1,0:T(8,128)(2,1)S(1)}, bf16[6,32,1024]{2,1,0:T(8,128)(2,1)S(1)}, u32[]{:S(2)}, u32[]{:S(2)}) collective-permute-start(bf16[6,32,1024]{2,1,0:T(8,128)(2,1)S(1)} %get-tuple-element.55), channel_id=1, source_target_pairs={{1,0},{2,1},{3,2},{5,4},{6,5},{7,6},{9,8},{10,9},{11,10},{13,12},{... | collective-permute-start | bytes 1179656 | tf_op jit(solution)/shard_map/ppermute | solution.py:482
  88.1 4.3 %collective-permute-start.15 = (bf16[96,512]{1,0:T(8,128)(2,1)S(1)}, bf16[96,512]{1,0:T(8,128)(2,1)S(1)}, u32[]{:S(2)}, u32[]{:S(2)}) collective-permute-start(bf16[96,512]{1,0:T(8,128)(2,1)S(1)} %get-tuple-element.66), channel_id=1, source_target_pairs={{0,3},{1,2},{2,1},{3,0},{4,7},{5,6},{6,5},{7,4},{8,11},{9,10},{10,... | collective-permute-start | bytes 294920 | tf_op jit(solution)/shard_map/ppermute | solution.py:250
  90.0 6.2 %collective-permute-start.14 = (bf16[96,512]{1,0:T(8,128)(2,1)S(1)}, bf16[96,512]{1,0:T(8,128)(2,1)S(1)}, u32[]{:S(2)}, u32[]{:S(2)}) collective-permute-start(bf16[96,512]{1,0:T(8,128)(2,1)S(1)} %get-tuple-element.66), channel_id=1, source_target_pairs={{0,2},{1,3},{2,0},{3,1},{4,6},{5,7},{6,4},{7,5},{8,10},{9,11},{10,... | collective-permute-start | bytes 294920 | tf_op jit(solution)/shard_map/ppermute | solution.py:250
  91.7 4.5 %collective-permute-start.13 = (bf16[96,512]{1,0:T(8,128)(2,1)S(1)}, bf16[96,512]{1,0:T(8,128)(2,1)S(1)}, u32[]{:S(2)}, u32[]{:S(2)}) collective-permute-start(bf16[96,512]{1,0:T(8,128)(2,1)S(1)} %get-tuple-element.66), channel_id=1, source_target_pairs={{0,1},{1,0},{2,3},{3,2},{4,5},{5,4},{6,7},{7,6},{8,9},{9,8},{10,11... | collective-permute-start | bytes 294920 | tf_op jit(solution)/shard_map/ppermute | solution.py:250
where the time goes:
time: 102 us; the launch traced here: 101 us
  Pallas kernels  43.1 us (42%)
  waiting for transfers between devices  34.3 us (34%)
  starting transfers between devices  22.4 us (22%)
    pallas_call x9, Pallas kernels, call(): pl.pallas_call(with_token, in_specs=specs, out_specs=tuple((VMEM for _ in...  43.1 us
    ppermute x3, waiting for transfers between devices, permute_groups(): return lax.ppermute(array, 'group', pairs)  24.4 us
    ppermute x9, waiting for transfers between devices, exchange(): lax.ppermute(half, 'grid', [(i, i ^ k) for i in range(GRID)])  9.89 us
    ppermute x9, starting transfers between devices, exchange(): lax.ppermute(half, 'grid', [(i, i ^ k) for i in range(GRID)])  7.98 us
    ppermute x3, starting transfers between devices, permute_groups(): return lax.ppermute(array, 'group', pairs)  7.22 us
    ppermute x1, starting transfers between devices, body(): lax.ppermute(high, 'grid', UP)  2.49 us
    ppermute x1, starting transfers between devices, body(): below = lax.ppermute(high, 'grid', UP)  2.08 us
  transfers between devices with their start and end apart: 16, of which 9 were waited for; matrix products, arithmetic and copies ran while one was open for 0% of the time, Pallas kernels for 25%

commit v1 on v0

--- a/solution.py
+++ b/solution.py
@@ -47,6 +47,7 @@
 MIB = 1 << 20
 PIECE = 32
 SCALE = 500e6
+EXTRA = 8
 CHUNKS = NCORE // PIECE
 NT = (((1,), (1,)), ((), ()))
 
@@ -266,7 +267,7 @@
         short = value.astype(BF16)
         if local_ref is not None:
             parts = [p.astype(F32) for p in split(local_ref[x : x + 1], 3)]
-            rest = jnp.zeros((12, PLANE), F32)
+            rest = jnp.zeros((EXTRA - 4, PLANE), F32)
             extra = jnp.concatenate(parts + [jnp.ones((1, PLANE), F32), rest], axis=0)
             short = jnp.concatenate([short, extra.astype(BF16)], axis=0)
         if x < HALO:
@@ -277,7 +278,7 @@
 
 def project(line, full, others, field, core_x, local):
     rows = field.shape[1]
-    sent = rows + (16 if local is not None else 0)
+    sent = rows + (EXTRA if local is not None else 0)
     return line.call(
         project_kernel,
         (
@@ -294,19 +295,23 @@
 DOWN = [(j, i) for i, j in UP]
 
 
-def filter_kernel(ahead, *refs):
+def filter_kernel(mode, offset, *refs):
     field_ref, below_ref, above_ref = refs[:3]
-    if ahead:
+    others = ()
+    if mode == "first":
         local_ref, weight_ref, first_ref, flag_ref, out_ref = refs[3:8]
+    elif mode == "more":
+        weight_ref, first_ref, flag_ref, out_ref = refs[3:7]
     else:
-        weight_ref, first_ref, flag_ref, core_ref, other_ref, out_ref, full_ref, half_ref = refs[3:11]
+        weight_ref, first_ref, flag_ref, core_ref = refs[3:7]
+        others, (out_ref, full_ref, half_ref) = refs[7:-7], refs[-7:-4]
     below, above, even, odd = refs[-4:]
     rows = field_ref.shape[1]
-    if ahead:
+    if mode == "first":
         weight_ref[HALO : HALO + SLAB] = 8.0 * local_ref[...] - 2.0
         for k, ref in enumerate((below_ref, above_ref)):
             for x in range(HALO):
-                extra = ref[x, rows : rows + 16, :].astype(F32)
+                extra = ref[x, rows : rows + EXTRA, :].astype(F32)
                 near = (extra[0:1] + extra[1:2]) + extra[2:3]
                 place = x if k == 0 else HALO + SLAB + x
                 weight_ref[place : place + 1] = 8.0 * near - 2.0
@@ -321,7 +326,7 @@
     def rolled(mask, value, by):
         return pltpu.roll(jnp.where(mask, 0.0, value), by % LANES, 1)
 
-    def sweep(local, at):
+    def sweep(local, at, put):
         def begin(x, lanes):
             if x < HALO:
                 return below[x, local, lanes]
@@ -363,14 +368,14 @@
                     elif x == HALO + SLAB:
                         value = value * high_flag
                     if k == KDEG:
-                        out_ref[x - HALO, at, lanes] = value * TOP
+                        out_ref[x - HALO, put, lanes] = value * TOP
                     else:
                         target[x, :, lanes] = value
             source = target
 
-    @pl.loop(0, rows // 16)
+    @pl.loop(0, out_ref.shape[1] // 16)
     def _(i):
-        both = pl.ds(pl.multiple_of(i * 16, 16), 16)
+        both = pl.ds(pl.multiple_of(offset + i * 16, 16), 16)
         below[...] = below_ref[:, both, :].astype(F32)
         above[...] = above_ref[:, both, :].astype(F32)
 
@@ -378,15 +383,16 @@
         def _(k):
             sweep(
                 pl.ds(pl.multiple_of(k * 8, 8), 8),
+                pl.ds(pl.multiple_of(offset + i * 16 + k * 8, 8), 8),
                 pl.ds(pl.multiple_of(i * 16 + k * 8, 8), 8),
             )
 
-    if not ahead:
-
-        def both_of(x):
-            return jnp.concatenate([other_ref[x].astype(BF16), out_ref[x].astype(BF16)], axis=0)
-
-        sums(both_of, core_ref, full_ref, half_ref)
+    if mode == "last":
+
+        def all_of(x):
+            return jnp.concatenate([r[x].astype(BF16) for r in (*others, out_ref)], axis=0)
+
+        sums(all_of, core_ref, full_ref, half_ref)
 
 
 def filter_scratch():
@@ -394,28 +400,36 @@
     return [halo, halo, whole, whole]
 
 
-def filter_ahead(line, field, below, above, local):
-    rows = field.shape[1]
+def filter_first(line, field, below, above, local):
     wide = struct((WIDE, PLANE), F32)
     got = line.call(
-        lambda *refs: filter_kernel(True, *refs),
-        (wide, wide, struct((2, 8, LANES), F32), struct((SLAB, rows, PLANE), F32)),
+        lambda *refs: filter_kernel("first", 0, *refs),
+        (wide, wide, struct((2, 8, LANES), F32), struct((SLAB, BATCH, PLANE), F32)),
         (field, below, above, local),
         scratch=filter_scratch(),
-        micros=7,
+        micros=6,
     )
     return got[:3], got[3]
 
 
-def filter_rest(line, field, below, above, weight, core_x, ahead):
-    rows = field.shape[1]
-    total = rows + ahead.shape[1]
-    return line.call(
-        lambda *refs: filter_kernel(False, *refs),
-        (struct((SLAB, rows, PLANE), F32), struct((total, NCORE), F32), struct((total, NCORE), BF16)),
-        (field, below, above, *weight, core_x, ahead),
+def filter_more(line, field, below, above, weight):
+    return line.call(
+        lambda *refs: filter_kernel("more", BATCH, *refs),
+        (struct((SLAB, BATCH, PLANE), F32),),
+        (field, below, above, *weight),
         scratch=filter_scratch(),
-        micros=14,
+        micros=6,
+    )[0]
+
+
+def filter_last(line, field, below, above, weight, core_x, others):
+    total = BATCH * (1 + len(others))
+    return line.call(
+        lambda *refs: filter_kernel("last", 0, *refs),
+        (struct((SLAB, BATCH, PLANE), F32), struct((total, NCORE), F32), struct((total, NCORE), BF16)),
+        (field, below, above, *weight, core_x, *others),
+        scratch=filter_scratch(),
+        micros=8,
     )
 
 
@@ -424,16 +438,19 @@
     return dot(parts[0], order_ref[...]) + dot(parts[1], order_ref[...])
 
 
-def clean_kernel(full_ref, a_ref, b_ref, c_ref, ahead_ref, rest_ref, mapped_ref, mapped_rest_ref, core_ref, order_ref, own_ref, density_ref, own, rows):
+def clean_kernel(full_ref, a_ref, b_ref, c_ref, first_ref, more_ref, last_ref, mapped_ref, mapped_rest_ref, core_ref, order_ref, own_ref, density_ref, own, rows):
     coef = total_of(full_ref, a_ref, b_ref, c_ref)
     for x in range(SLAB):
         taken = dot(coef, core_ref[x])
-        ahead = ahead_ref[x] - taken[: ahead_ref.shape[1]]
-        rest = rest_ref[x] - taken[ahead_ref.shape[1] :]
-        own[x * BATCH : (x + 1) * BATCH] = ahead[:BATCH]
-        weighted = jnp.sum(mapped_ref[x].astype(F32) * ahead, axis=0, keepdims=True)
-        weighted += jnp.sum(mapped_rest_ref[x].astype(F32) * rest, axis=0, keepdims=True)
-        rows[x : x + 1] = weighted / (3.0 * BATCH)
+        mapped = (mapped_ref[x, :BATCH], mapped_ref[x, BATCH:], mapped_rest_ref[x])
+        total = None
+        for t, ref in enumerate((first_ref, more_ref, last_ref)):
+            value = ref[x] - taken[t * BATCH : (t + 1) * BATCH]
+            if t == 0:
+                own[x * BATCH : (x + 1) * BATCH] = value
+            term = mapped[t].astype(F32) * value
+            total = term if total is None else total + term
+        rows[x : x + 1] = jnp.sum(total, axis=0, keepdims=True) / (3.0 * BATCH)
     back = row_permutation(BATCH * SLAB, BATCH)
     total = None
     for part in split(own[...], 2):
@@ -443,12 +460,12 @@
     density_ref[...] = reorder(rows[...], order_ref)
 
 
-def clean(line, full, others, ahead, rest, mapped, mapped_rest, core_x, order):
+def clean(line, full, others, fields, mapped, mapped_rest, core_x, order):
     small, own = struct((SLAB, PLANE), F32), struct((SLAB * BATCH, PLANE), F32)
     return line.call(
         clean_kernel,
         (own, small),
-        (full, *others, ahead, rest, mapped, mapped_rest, core_x, order),
+        (full, *others, *fields, mapped, mapped_rest, core_x, order),
         scratch=[pltpu.VMEM(own.shape, F32), pltpu.VMEM(small.shape, F32)],
         limit=12,
         micros=4,
@@ -478,14 +495,16 @@
 
     mapped_rest, full, half = map_batches(line, pick, core_x, [(mate, second)])
     others = exchange(half)
+    weight, first = filter_first(line, field, below, above, local)
     rest, low, high = project(line, full, others, mapped_rest, core_x, None)
-    below_rest, above_rest = lax.ppermute(high, "grid", UP), lax.ppermute(low, "grid", DOWN)
-
-    weight, ahead = filter_ahead(line, field, below, above, local)
-    rest, full, half = filter_rest(line, rest, below_rest, above_rest, weight, core_x, ahead)
-    own, density = clean(
-        line, full, exchange(half), ahead, rest, mapped, mapped_rest, core_x, order
-    )
+    below_rest = lax.ppermute(high, "grid", UP)
+    above_rest = lax.ppermute(low, "grid", DOWN)
+    more = filter_more(line, field, below, above, weight)
+    last, full, half = filter_last(
+        line, rest, below_rest, above_rest, weight, core_x, (first, more)
+    )
+    fields = (first, more, last)
+    own, density = clean(line, full, exchange(half), fields, mapped, mapped_rest, core_x, order)
     return density[None], own.reshape(BATCH, SLAB, PLANE)
 
 

time: 102 us -> 100 us (0.980); the launches traced: 101 us -> 99.8 us
  waiting for transfers between devices: 34.3 us -> 31.8 us
  starting transfers between devices: 22.4 us -> 24 us
    ppermute x9, waiting for transfers between devices: 9.89 us -> 7.42 us  [exchange(): lax.ppermute(half, 'grid', [(i, i ^ k) for i in range(GRID)])]
    ppermute x9, starting transfers between devices: 7.98 us -> 9.69 us  [exchange(): lax.ppermute(half, 'grid', [(i, i ^ k) for i in range(GRID)])]
    pallas_call x9 -> x10, Pallas kernels: 43.1 us -> 43.1 us  [call(): pl.pallas_call(with_token, in_specs=specs, out_specs=tuple((VMEM for _ in...]
  transfers between devices with their start and end apart: 16 -> 16, of which waited for: 9 -> 6; matrix products, arithmetic and copies ran while one was open for 0% -> 0% of each run, Pallas kernels for 25% -> 23%
where the time goes in v1:
time: 100 us; the launch traced here: 99.8 us
  Pallas kernels  43.1 us (43%)
  waiting for transfers between devices  31.8 us (32%)
  starting transfers between devices  24 us (24%)
    pallas_call x10, Pallas kernels, call(): pl.pallas_call(with_token, in_specs=specs, out_specs=tuple((VMEM for _ in...  43.1 us
    ppermute x3, waiting for transfers between devices, permute_groups(): return lax.ppermute(array, 'group', pairs)  24.4 us
    ppermute x9, starting transfers between devices, exchange(): lax.ppermute(half, 'grid', [(i, i ^ k) for i in range(GRID)])  9.69 us
    ppermute x9, waiting for transfers between devices, exchange(): lax.ppermute(half, 'grid', [(i, i ^ k) for i in range(GRID)])  7.42 us
    ppermute x3, starting transfers between devices, permute_groups(): return lax.ppermute(array, 'group', pairs)  7.22 us
    ppermute x1, starting transfers between devices, body(): below_rest = lax.ppermute(high, 'grid', UP)  2.41 us
    ppermute x1, starting transfers between devices, body(): below = lax.ppermute(high, 'grid', UP)  2.08 us
  transfers between devices with their start and end apart: 16, of which 6 were waited for; matrix products, arithmetic and copies ran while one was open for 0% of the time, Pallas kernels for 23%

profile of v1, /device:TPU:0, one launch (start us, length us, event | category | flops | bytes accessed | tf_op | source)
XLA Modules:
  0.0 99.8 jit_solution(9411717941134865056)
XLA Ops:
  0.6 3.4 %collective-permute-start = (bf16[32,8,1024]{2,1,0:T(8,128)(2,1)}, bf16[32,8,1024]{2,1,0:T(8,128)(2,1)S(1)}, u32[]{:S(2)}, u32[]{:S(2)}) collective-permute-start(bf16[32,8,1024]{2,1,0:T(8,128)(2,1)} %param.4), channel_id=1, source_target_pairs={{0,4},{4,0},{8,12},{12,8},{16,20},{20,16},{24,28},{28,24},{32,36},... | collective-permute-start | bytes 1572872 | tf_op jit(solution)/shard_map/ppermute | solution.py:476
  4.0 1.9 %collective-permute-start.2 = (bf16[32,8,1024]{2,1,0:T(8,128)(2,1)}, bf16[32,8,1024]{2,1,0:T(8,128)(2,1)S(1)}, u32[]{:S(2)}, u32[]{:S(2)}) collective-permute-start(bf16[32,8,1024]{2,1,0:T(8,128)(2,1)} %param.4), channel_id=1, source_target_pairs={{0,8},{4,12},{8,16},{12,20},{16,24},{20,28},{24,32},{28,36},{32,40... | collective-permute-start | bytes 1572872 | tf_op jit(solution)/shard_map/ppermute | solution.py:476
  5.9 0.0 copy-start.1
  5.9 0.0 copy-start.2
  5.9 7.2 %shard_map.59 = (bf16[8,512,1024]{2,1,0:T(8,128)(2,1)S(1)}, f32[8,128]{1,0:T(8,128)S(1)}) custom-call(bf16[4096,1024]{1,0:T(8,128)(2,1)} %bitcast.13), custom_call_target="tpu_custom_call" | custom-call | flops 4000000000 | bytes 1024 | tf_op jit(solution)/shard_map/pallas_call | solution.py:74
  13.1 0.0 copy-start
  13.2 0.0 copy-done.1
  13.2 0.0 copy-done.2
  13.2 1.8 %shard_map.60 = (bf16[1024,1024]{1,0:T(8,128)(2,1)S(1)}, bf16[1024,1024]{1,0:T(8,128)(2,1)S(1)}, f32[8,1024]{1,0:T(8,128)S(1)}, f32[8,128]{1,0:T(8,128)S(1)}) custom-call(s32[1,1024]{1,0:T(1,128)S(1)} %copy-done.2, f32[8,1024]{1,0:T(8,128)S(1)} %bitcast.12, f32[8,128]{1,0:T(8,128)S(1)} %get-tuple-element.39.refs_2_), custom_call_target="tpu_custom_call" | custom-call | flops 1000000000 | bytes 1024 | tf_op jit(solution)/shard_map/pallas_call | solution.py:74
  15.0 1.1 %collective-permute-done = bf16[32,8,1024]{2,1,0:T(8,128)(2,1)S(1)} collective-permute-done((bf16[32,8,1024]{2,1,0:T(8,128)(2,1)}, bf16[32,8,1024]{2,1,0:T(8,128)(2,1)S(1)}, u32[]{:S(2)}, u32[]{:S(2)}) %collective-permute-start) | collective-permute-done | bytes 524320 | tf_op jit(solution)/shard_map/ppermute | solution.py:476
  16.2 6.0 %collective-permute-done.2 = bf16[32,8,1024]{2,1,0:T(8,128)(2,1)S(1)} collective-permute-done((bf16[32,8,1024]{2,1,0:T(8,128)(2,1)}, bf16[32,8,1024]{2,1,0:T(8,128)(2,1)S(1)}, u32[]{:S(2)}, u32[]{:S(2)}) %collective-permute-start.2) | collective-permute-done | bytes 524320 | tf_op jit(solution)/shard_map/ppermute | solution.py:476
  22.1 0.0 copy-done
  22.1 4.0 %shard_map.61 = (bf16[8,64,1024]{2,1,0:T(8,128)(2,1)S(1)}, f32[64,512]{1,0:T(8,128)S(1)}, bf16[64,512]{1,0:T(8,128)(2,1)S(1)}, f32[8,128]{1,0:T(8,128)S(1)}) custom-call(bf16[1024,1024]{1,0:T(8,128)(2,1)S(1)} %get-tuple-element.40.refs_0_, bf16[8,512,1024]{2,1,0:T(8,128)(2,1)S(1)} %get-tuple-element.41.refs_1_.refs_5_.refs_6_.refs_9_, ...), custom_call_target="tpu_custom_call" | custom-call | flops 1500000000 | bytes 1024 | tf_op jit(solution)/shard_map/pallas_call | solution.py:74
  26.2 0.1 collective-permute-start.5
  26.3 0.8 collective-permute-start.4
  27.0 1.1 %collective-permute-start.3 = (bf16[64,512]{1,0:T(8,128)(2,1)S(1)}, bf16[64,512]{1,0:T(8,128)(2,1)S(1)}, u32[]{:S(2)}, u32[]{:S(2)}) collective-permute-start(bf16[64,512]{1,0:T(8,128)(2,1)S(1)} %get-tuple-element.46), channel_id=1, source_target_pairs={{0,1},{1,0},{2,3},{3,2},{4,5},{5,4},{6,7},{7,6},{8,9},{9,8},{10,11... | collective-permute-start | bytes 196616 | tf_op jit(solution)/shard_map/ppermute | solution.py:251
  28.1 1.9 %collective-permute-done.5.refs_3_ = bf16[64,512]{1,0:T(8,128)(2,1)S(1)} collective-permute-done((bf16[64,512]{1,0:T(8,128)(2,1)S(1)}, bf16[64,512]{1,0:T(8,128)(2,1)S(1)}, u32[]{:S(2)}, u32[]{:S(2)}) %collective-permute-start.5) | collective-permute-done | bytes 65568 | tf_op jit(solution)/shard_map/ppermute | solution.py:251
  30.0 1.3 %collective-permute-done.4.refs_2_ = bf16[64,512]{1,0:T(8,128)(2,1)S(1)} collective-permute-done((bf16[64,512]{1,0:T(8,128)(2,1)S(1)}, bf16[64,512]{1,0:T(8,128)(2,1)S(1)}, u32[]{:S(2)}, u32[]{:S(2)}) %collective-permute-start.4) | collective-permute-done | bytes 65568 | tf_op jit(solution)/shard_map/ppermute | solution.py:251
  31.3 0.0 collective-permute-done.3.refs_1_
  31.3 1.6 %shard_map.62 = (f32[8,64,1024]{2,1,0:T(8,128)S(1)}, bf16[6,72,1024]{2,1,0:T(8,128)(2,1)S(1)}, bf16[6,72,1024]{2,1,0:T(8,128)(2,1)S(1)}, f32[8,128]{1,0:T(8,128)S(1)}) custom-call(f32[64,512]{1,0:T(8,128)S(1)} %get-tuple-element.45.refs_0_, bf16[64,512]{1,0:T(8,128)(2,1)S(1)} %collective-permute-done.3.refs_1_, ...), custom_call_target="tpu_custom_call" | custom-call | flops 1000000000 | bytes 1024 | tf_op jit(solution)/shard_map/pallas_call | solution.py:74
  32.9 2.1 %collective-permute-start.9 = (bf16[6,72,1024]{2,1,0:T(8,128)(2,1)S(1)}, bf16[6,72,1024]{2,1,0:T(8,128)(2,1)S(1)}, u32[]{:S(2)}, u32[]{:S(2)}) collective-permute-start(bf16[6,72,1024]{2,1,0:T(8,128)(2,1)S(1)} %get-tuple-element.55), channel_id=1, source_target_pairs={{0,1},{1,2},{2,3},{4,5},{5,6},{6,7},{8,9},{9,10},{10,11},{12,13},{... | collective-permute-start | bytes 2654216 | tf_op jit(solution)/shard_map/ppermute | solution.py:493
  35.0 1.3 %collective-permute-start.10 = (bf16[6,72,1024]{2,1,0:T(8,128)(2,1)S(1)}, bf16[6,72,1024]{2,1,0:T(8,128)(2,1)S(1)}, u32[]{:S(2)}, u32[]{:S(2)}) collective-permute-start(bf16[6,72,1024]{2,1,0:T(8,128)(2,1)S(1)} %get-tuple-element.56), channel_id=1, source_target_pairs={{1,0},{2,1},{3,2},{5,4},{6,5},{7,6},{9,8},{10,9},{11,10},{13,12},{... | collective-permute-start | bytes 2654216 | tf_op jit(solution)/shard_map/ppermute | solution.py:494
  36.3 1.9 %collective-permute-start.1 = (bf16[32,8,1024]{2,1,0:T(8,128)(2,1)S(1)}, bf16[32,8,1024]{2,1,0:T(8,128)(2,1)S(1)}, u32[]{:S(2)}, u32[]{:S(2)}) collective-permute-start(bf16[32,8,1024]{2,1,0:T(8,128)(2,1)S(1)} %collective-permute-done), channel_id=1, source_target_pairs={{0,8},{8,16},{16,24},{24,32},{32,40},{40,48},{48,56},{56,64},{64,7... | collective-permute-start | bytes 1572872 | tf_op jit(solution)/shard_map/ppermute | solution.py:476
  38.2 17.3 %collective-permute-done.1 = bf16[32,8,1024]{2,1,0:T(8,128)(2,1)S(1)} collective-permute-done((bf16[32,8,1024]{2,1,0:T(8,128)(2,1)S(1)}, bf16[32,8,1024]{2,1,0:T(8,128)(2,1)S(1)}, u32[]{:S(2)}, u32[]{:S(2)}) %collective-permute-start.1) | collective-permute-done | bytes 524320 | tf_op jit(solution)/shard_map/ppermute | solution.py:476
  55.5 3.3 %shard_map.63 = (bf16[8,32,1024]{2,1,0:T(8,128)(2,1)S(1)}, f32[32,512]{1,0:T(8,128)S(1)}, bf16[32,512]{1,0:T(8,128)(2,1)S(1)}, f32[8,128]{1,0:T(8,128)S(1)}) custom-call(bf16[1024,1024]{1,0:T(8,128)(2,1)S(1)} %get-tuple-element.40.refs_0_, bf16[8,512,1024]{2,1,0:T(8,128)(2,1)S(1)} %get-tuple-element.41.refs_1_.refs_5_.refs_6_.refs_9_, ...), custom_call_target="tpu_custom_call" | custom-call | flops 1000000000 | bytes 1024 | tf_op jit(solution)/shard_map/pallas_call | solution.py:74
  58.7 0.0 collective-permute-start.8
  58.8 2.3 %collective-permute-start.7 = (bf16[32,512]{1,0:T(8,128)(2,1)S(1)}, bf16[32,512]{1,0:T(8,128)(2,1)S(1)}, u32[]{:S(2)}, u32[]{:S(2)}) collective-permute-start(bf16[32,512]{1,0:T(8,128)(2,1)S(1)} %get-tuple-element.52), channel_id=1, source_target_pairs={{0,2},{1,3},{2,0},{3,1},{4,6},{5,7},{6,4},{7,5},{8,10},{9,11},{10,... | collective-permute-start | bytes 98312 | tf_op jit(solution)/shard_map/ppermute | solution.py:251
  61.1 0.0 collective-permute-start.6
  61.1 0.0 collective-permute-done.9.refs_1_
  61.1 0.0 collective-permute-done.10.refs_2_
  61.1 5.5 %shard_map.64 = (f32[20,1024]{1,0:T(8,128)S(1)}, f32[20,1024]{1,0:T(8,128)S(1)}, f32[2,8,128]{2,1,0:T(8,128)S(1)}, f32[8,32,1024]{2,1,0:T(8,128)S(1)}, f32[8,128]{1,0:T(8,128)S(1)}) custom-call(f32[8,64,1024]{2,1,0:T(8,128)S(1)} %get-tuple-element.54.refs_0_, bf16[6,72,1024]{2,1,0:T(8,128)(2,1)S(1)} %collective-permute-done.9.refs_1_, ...), custom_call_target="tpu_custom_call" | custom-call | flops 3000000000 | bytes 1024 | tf_op jit(solution)/shard_map/pallas_call | solution.py:74
  66.7 0.0 collective-permute-done.8.refs_3_
  66.7 0.0 collective-permute-done.7.refs_2_
  66.7 0.0 collective-permute-done.6.refs_1_
  66.7 1.6 %shard_map.65 = (f32[8,32,1024]{2,1,0:T(8,128)S(1)}, bf16[6,32,1024]{2,1,0:T(8,128)(2,1)S(1)}, bf16[6,32,1024]{2,1,0:T(8,128)(2,1)S(1)}, f32[8,128]{1,0:T(8,128)S(1)}) custom-call(f32[32,512]{1,0:T(8,128)S(1)} %get-tuple-element.51.refs_0_, bf16[32,512]{1,0:T(8,128)(2,1)S(1)} %collective-permute-done.6.refs_1_, ...), custom_call_target="tpu_custom_call" | custom-call | flops 1000000000 | bytes 1024 | tf_op jit(solution)/shard_map/pallas_call | solution.py:74
  68.3 2.4 %collective-permute-start.11 = (bf16[6,32,1024]{2,1,0:T(8,128)(2,1)S(1)}, bf16[6,32,1024]{2,1,0:T(8,128)(2,1)S(1)}, u32[]{:S(2)}, u32[]{:S(2)}) collective-permute-start(bf16[6,32,1024]{2,1,0:T(8,128)(2,1)S(1)} %get-tuple-element.60), channel_id=1, source_target_pairs={{0,1},{1,2},{2,3},{4,5},{5,6},{6,7},{8,9},{9,10},{10,11},{12,13},{... | collective-permute-start | bytes 1179656 | tf_op jit(solution)/shard_map/ppermute | solution.py:500
  70.7 1.3 %collective-permute-start.12 = (bf16[6,32,1024]{2,1,0:T(8,128)(2,1)S(1)}, bf16[6,32,1024]{2,1,0:T(8,128)(2,1)S(1)}, u32[]{:S(2)}, u32[]{:S(2)}) collective-permute-start(bf16[6,32,1024]{2,1,0:T(8,128)(2,1)S(1)} %get-tuple-element.61), channel_id=1, source_target_pairs={{1,0},{2,1},{3,2},{5,4},{6,5},{7,6},{9,8},{10,9},{11,10},{13,12},{... | collective-permute-start | bytes 1179656 | tf_op jit(solution)/shard_map/ppermute | solution.py:501
  72.0 5.4 %shard_map.66 = (f32[8,32,1024]{2,1,0:T(8,128)S(1)}, f32[8,128]{1,0:T(8,128)S(1)}) custom-call(f32[8,64,1024]{2,1,0:T(8,128)S(1)} %get-tuple-element.54.refs_0_, bf16[6,72,1024]{2,1,0:T(8,128)(2,1)S(1)} %collective-permute-done.9.refs_1_, bf16[6,72,1024]{2,1,0:T(8,128)(2,1)S(1)} %collective-permute-done.10.refs_2_, ...), custom_call_target="tpu_custom_call" | custom-call | flops 3000000000 | bytes 1024 | tf_op jit(solution)/shard_map/pallas_call | solution.py:74
  77.4 0.0 collective-permute-done.11.refs_1_
  77.4 0.0 collective-permute-done.12.refs_2_
  77.4 8.4 %shard_map.67 = (f32[8,32,1024]{2,1,0:T(8,128)S(1)}, f32[96,512]{1,0:T(8,128)S(1)}, bf16[96,512]{1,0:T(8,128)(2,1)S(1)}, f32[8,128]{1,0:T(8,128)S(1)}) custom-call(f32[8,32,1024]{2,1,0:T(8,128)S(1)} %get-tuple-element.59.refs_0_, bf16[6,32,1024]{2,1,0:T(8,128)(2,1)S(1)} %collective-permute-done.11.refs_1_, ...), custom_call_target="tpu_custom_call" | custom-call | flops 4000000000 | bytes 1024 | tf_op jit(solution)/shard_map/pallas_call | solution.py:74
  85.9 2.1 %collective-permute-start.15 = (bf16[96,512]{1,0:T(8,128)(2,1)S(1)}, bf16[96,512]{1,0:T(8,128)(2,1)S(1)}, u32[]{:S(2)}, u32[]{:S(2)}) collective-permute-start(bf16[96,512]{1,0:T(8,128)(2,1)S(1)} %get-tuple-element.70), channel_id=1, source_target_pairs={{0,3},{1,2},{2,1},{3,0},{4,7},{5,6},{6,5},{7,4},{8,11},{9,10},{10,... | collective-permute-start | bytes 294920 | tf_op jit(solution)/shard_map/ppermute | solution.py:251
  87.9 3.3 %collective-permute-start.14 = (bf16[96,512]{1,0:T(8,128)(2,1)S(1)}, bf16[96,512]{1,0:T(8,128)(2,1)S(1)}, u32[]{:S(2)}, u32[]{:S(2)}) collective-permute-start(bf16[96,512]{1,0:T(8,128)(2,1)S(1)} %get-tuple-element.70), channel_id=1, source_target_pairs={{0,2},{1,3},{2,0},{3,1},{4,6},{5,7},{6,4},{7,5},{8,10},{9,11},{10,... | collective-permute-start | bytes 294920 | tf_op jit(solution)/shard_map/ppermute | solution.py:251
  91.2 0.0 collective-permute-start.13
  91.2 0.0 collective-permute-done.15.refs_3_
  91.3 4.2 %collective-permute-done.14.refs_2_ = bf16[96,512]{1,0:T(8,128)(2,1)S(1)} collective-permute-done((bf16[96,512]{1,0:T(8,128)(2,1)S(1)}, bf16[96,512]{1,0:T(8,128)(2,1)S(1)}, u32[]{:S(2)}, u32[]{:S(2)}) %collective-permute-start.14) | collective-permute-done | bytes 98336 | tf_op jit(solution)/shard_map/ppermute | solution.py:251
  95.5 0.0 collective-permute-done.13.refs_1_
  95.5 4.3 %shard_map.68 = (f32[256,1024]{1,0:T(8,128)}, f32[8,1024]{1,0:T(8,128)}, f32[8,128]{1,0:T(8,128)}) custom-call(f32[96,512]{1,0:T(8,128)S(1)} %get-tuple-element.69.refs_0_, bf16[96,512]{1,0:T(8,128)(2,1)S(1)} %collective-permute-done.13.refs_1_, bf16[96,512]{1,0:T(8,128)(2,1)S(1)} %collective-permute-done.14.refs_2_, ...), custom_call_target="tpu_custom_call" | custom-call | flops 2000000000 | bytes 1024 | tf_op jit(solution)/shard_map/pallas_call | solution.py:74
Async XLA Ops:
  0.6 15.5 %collective-permute-start = (bf16[32,8,1024]{2,1,0:T(8,128)(2,1)}, bf16[32,8,1024]{2,1,0:T(8,128)(2,1)S(1)}, u32[]{:S(2)}, u32[]{:S(2)}) collective-permute-start(bf16[32,8,1024]{2,1,0:T(8,128)(2,1)} %param.4), channel_id=1, source_target_pairs={{0,4},{4,0},{8,12},{12,8},{16,20},{20,16},{24,28},{28,24},{32,36},... | collective-permute-start | bytes 1572872 | tf_op jit(solution)/shard_map/ppermute | solution.py:476
  4.0 18.1 %collective-permute-start.2 = (bf16[32,8,1024]{2,1,0:T(8,128)(2,1)}, bf16[32,8,1024]{2,1,0:T(8,128)(2,1)S(1)}, u32[]{:S(2)}, u32[]{:S(2)}) collective-permute-start(bf16[32,8,1024]{2,1,0:T(8,128)(2,1)} %param.4), channel_id=1, source_target_pairs={{0,8},{4,12},{8,16},{12,20},{16,24},{20,28},{24,32},{28,36},{32,40... | collective-permute-start | bytes 1572872 | tf_op jit(solution)/shard_map/ppermute | solution.py:476
  5.9 7.2 %copy-start.1 = (f32[1,8,1024]{2,1,0:T(8,128)S(1)}, f32[1,8,1024]{2,1,0:T(8,128)}, u32[]{:S(2)}) copy-start(f32[1,8,1024]{2,1,0:T(8,128)} %param.7) | copy-start | bytes 98308
  5.9 7.2 %copy-start.2 = (s32[1,1024]{1,0:T(1,128)S(1)}, s32[1,1024]{1,0:T(1,128)}, u32[]{:S(2)}) copy-start(s32[1,1024]{1,0:T(1,128)} %refs_0_.1) | copy-start | bytes 12292
  13.1 9.0 %copy-start = (bf16[32,8,1024]{2,1,0:T(8,128)(2,1)S(1)}, bf16[32,8,1024]{2,1,0:T(8,128)(2,1)}, u32[]{:S(2)}) copy-start(bf16[32,8,1024]{2,1,0:T(8,128)(2,1)} %param.4) | copy-start | bytes 1572868
  26.2 3.8 %collective-permute-start.5 = (bf16[64,512]{1,0:T(8,128)(2,1)S(1)}, bf16[64,512]{1,0:T(8,128)(2,1)S(1)}, u32[]{:S(2)}, u32[]{:S(2)}) collective-permute-start(bf16[64,512]{1,0:T(8,128)(2,1)S(1)} %get-tuple-element.46), channel_id=1, source_target_pairs={{0,3},{1,2},{2,1},{3,0},{4,7},{5,6},{6,5},{7,4},{8,11},{9,10},{10,... | collective-permute-start | bytes 196616 | tf_op jit(solution)/shard_map/ppermute | solution.py:251
  26.3 5.0 %collective-permute-start.4 = (bf16[64,512]{1,0:T(8,128)(2,1)S(1)}, bf16[64,512]{1,0:T(8,128)(2,1)S(1)}, u32[]{:S(2)}, u32[]{:S(2)}) collective-permute-start(bf16[64,512]{1,0:T(8,128)(2,1)S(1)} %get-tuple-element.46), channel_id=1, source_target_pairs={{0,2},{1,3},{2,0},{3,1},{4,6},{5,7},{6,4},{7,5},{8,10},{9,11},{10,... | collective-permute-start | bytes 196616 | tf_op jit(solution)/shard_map/ppermute | solution.py:251
  27.0 4.3 %collective-permute-start.3 = (bf16[64,512]{1,0:T(8,128)(2,1)S(1)}, bf16[64,512]{1,0:T(8,128)(2,1)S(1)}, u32[]{:S(2)}, u32[]{:S(2)}) collective-permute-start(bf16[64,512]{1,0:T(8,128)(2,1)S(1)} %get-tuple-element.46), channel_id=1, source_target_pairs={{0,1},{1,0},{2,3},{3,2},{4,5},{5,4},{6,7},{7,6},{8,9},{9,8},{10,11... | collective-permute-start | bytes 196616 | tf_op jit(solution)/shard_map/ppermute | solution.py:251
  32.9 28.2 %collective-permute-start.9 = (bf16[6,72,1024]{2,1,0:T(8,128)(2,1)S(1)}, bf16[6,72,1024]{2,1,0:T(8,128)(2,1)S(1)}, u32[]{:S(2)}, u32[]{:S(2)}) collective-permute-start(bf16[6,72,1024]{2,1,0:T(8,128)(2,1)S(1)} %get-tuple-element.55), channel_id=1, source_target_pairs={{0,1},{1,2},{2,3},{4,5},{5,6},{6,7},{8,9},{9,10},{10,11},{12,13},{... | collective-permute-start | bytes 2654216 | tf_op jit(solution)/shard_map/ppermute | solution.py:493
  35.0 26.1 %collective-permute-start.10 = (bf16[6,72,1024]{2,1,0:T(8,128)(2,1)S(1)}, bf16[6,72,1024]{2,1,0:T(8,128)(2,1)S(1)}, u32[]{:S(2)}, u32[]{:S(2)}) collective-permute-start(bf16[6,72,1024]{2,1,0:T(8,128)(2,1)S(1)} %get-tuple-element.56), channel_id=1, source_target_pairs={{1,0},{2,1},{3,2},{5,4},{6,5},{7,6},{9,8},{10,9},{11,10},{13,12},{... | collective-permute-start | bytes 2654216 | tf_op jit(solution)/shard_map/ppermute | solution.py:494
  36.3 19.2 %collective-permute-start.1 = (bf16[32,8,1024]{2,1,0:T(8,128)(2,1)S(1)}, bf16[32,8,1024]{2,1,0:T(8,128)(2,1)S(1)}, u32[]{:S(2)}, u32[]{:S(2)}) collective-permute-start(bf16[32,8,1024]{2,1,0:T(8,128)(2,1)S(1)} %collective-permute-done), channel_id=1, source_target_pairs={{0,8},{8,16},{16,24},{24,32},{32,40},{40,48},{48,56},{56,64},{64,7... | collective-permute-start | bytes 1572872 | tf_op jit(solution)/shard_map/ppermute | solution.py:476
  58.7 7.9 %collective-permute-start.8 = (bf16[32,512]{1,0:T(8,128)(2,1)S(1)}, bf16[32,512]{1,0:T(8,128)(2,1)S(1)}, u32[]{:S(2)}, u32[]{:S(2)}) collective-permute-start(bf16[32,512]{1,0:T(8,128)(2,1)S(1)} %get-tuple-element.52), channel_id=1, source_target_pairs={{0,3},{1,2},{2,1},{3,0},{4,7},{5,6},{6,5},{7,4},{8,11},{9,10},{10,... | collective-permute-start | bytes 98312 | tf_op jit(solution)/shard_map/ppermute | solution.py:251
  58.8 7.9 %collective-permute-start.7 = (bf16[32,512]{1,0:T(8,128)(2,1)S(1)}, bf16[32,512]{1,0:T(8,128)(2,1)S(1)}, u32[]{:S(2)}, u32[]{:S(2)}) collective-permute-start(bf16[32,512]{1,0:T(8,128)(2,1)S(1)} %get-tuple-element.52), channel_id=1, source_target_pairs={{0,2},{1,3},{2,0},{3,1},{4,6},{5,7},{6,4},{7,5},{8,10},{9,11},{10,... | collective-permute-start | bytes 98312 | tf_op jit(solution)/shard_map/ppermute | solution.py:251
  61.1 5.6 %collective-permute-start.6 = (bf16[32,512]{1,0:T(8,128)(2,1)S(1)}, bf16[32,512]{1,0:T(8,128)(2,1)S(1)}, u32[]{:S(2)}, u32[]{:S(2)}) collective-permute-start(bf16[32,512]{1,0:T(8,128)(2,1)S(1)} %get-tuple-element.52), channel_id=1, source_target_pairs={{0,1},{1,0},{2,3},{3,2},{4,5},{5,4},{6,7},{7,6},{8,9},{9,8},{10,11... | collective-permute-start | bytes 98312 | tf_op jit(solution)/shard_map/ppermute | solution.py:251
  68.3 9.2 %collective-permute-start.11 = (bf16[6,32,1024]{2,1,0:T(8,128)(2,1)S(1)}, bf16[6,32,1024]{2,1,0:T(8,128)(2,1)S(1)}, u32[]{:S(2)}, u32[]{:S(2)}) collective-permute-start(bf16[6,32,1024]{2,1,0:T(8,128)(2,1)S(1)} %get-tuple-element.60), channel_id=1, source_target_pairs={{0,1},{1,2},{2,3},{4,5},{5,6},{6,7},{8,9},{9,10},{10,11},{12,13},{... | collective-permute-start | bytes 1179656 | tf_op jit(solution)/shard_map/ppermute | solution.py:500
  70.7 6.8 %collective-permute-start.12 = (bf16[6,32,1024]{2,1,0:T(8,128)(2,1)S(1)}, bf16[6,32,1024]{2,1,0:T(8,128)(2,1)S(1)}, u32[]{:S(2)}, u32[]{:S(2)}) collective-permute-start(bf16[6,32,1024]{2,1,0:T(8,128)(2,1)S(1)} %get-tuple-element.61), channel_id=1, source_target_pairs={{1,0},{2,1},{3,2},{5,4},{6,5},{7,6},{9,8},{10,9},{11,10},{13,12},{... | collective-permute-start | bytes 1179656 | tf_op jit(solution)/shard_map/ppermute | solution.py:501
  85.9 5.4 %collective-permute-start.15 = (bf16[96,512]{1,0:T(8,128)(2,1)S(1)}, bf16[96,512]{1,0:T(8,128)(2,1)S(1)}, u32[]{:S(2)}, u32[]{:S(2)}) collective-permute-start(bf16[96,512]{1,0:T(8,128)(2,1)S(1)} %get-tuple-element.70), channel_id=1, source_target_pairs={{0,3},{1,2},{2,1},{3,0},{4,7},{5,6},{6,5},{7,4},{8,11},{9,10},{10,... | collective-permute-start | bytes 294920 | tf_op jit(solution)/shard_map/ppermute | solution.py:251
  87.9 7.5 %collective-permute-start.14 = (bf16[96,512]{1,0:T(8,128)(2,1)S(1)}, bf16[96,512]{1,0:T(8,128)(2,1)S(1)}, u32[]{:S(2)}, u32[]{:S(2)}) collective-permute-start(bf16[96,512]{1,0:T(8,128)(2,1)S(1)} %get-tuple-element.70), channel_id=1, source_target_pairs={{0,2},{1,3},{2,0},{3,1},{4,6},{5,7},{6,4},{7,5},{8,10},{9,11},{10,... | collective-permute-start | bytes 294920 | tf_op jit(solution)/shard_map/ppermute | solution.py:251
  91.2 4.2 %collective-permute-start.13 = (bf16[96,512]{1,0:T(8,128)(2,1)S(1)}, bf16[96,512]{1,0:T(8,128)(2,1)S(1)}, u32[]{:S(2)}, u32[]{:S(2)}) collective-permute-start(bf16[96,512]{1,0:T(8,128)(2,1)S(1)} %get-tuple-element.70), channel_id=1, source_target_pairs={{0,1},{1,0},{2,3},{3,2},{4,5},{5,4},{6,7},{7,6},{8,9},{9,8},{10,11... | collective-permute-start | bytes 294920 | tf_op jit(solution)/shard_map/ppermute | solution.py:251

commit v2 on v1

--- a/solution.py
+++ b/solution.py
@@ -258,34 +258,34 @@
 
 
 def project_kernel(full_ref, a_ref, b_ref, c_ref, field_ref, core_ref, *refs):
-    local_ref = refs[0] if len(refs) == 4 else None
-    out_ref, low_ref, high_ref = refs[-3:]
+    split_up = len(refs) == 6
+    local_ref = refs[0] if split_up else None
+    out_ref, halos = (refs[1], refs[2:]) if split_up else (refs[0], refs[1:])
     coef = total_of(full_ref, a_ref, b_ref, c_ref)
     for x in range(SLAB):
         value = field_ref[x].astype(F32) - dot(coef, core_ref[x])
         out_ref[x] = value
-        short = value.astype(BF16)
-        if local_ref is not None:
+        sent = [value.astype(BF16)]
+        if split_up:
             parts = [p.astype(F32) for p in split(local_ref[x : x + 1], 3)]
             rest = jnp.zeros((EXTRA - 4, PLANE), F32)
             extra = jnp.concatenate(parts + [jnp.ones((1, PLANE), F32), rest], axis=0)
-            short = jnp.concatenate([short, extra.astype(BF16)], axis=0)
-        if x < HALO:
-            low_ref[x] = short
-        if x >= SLAB - HALO:
-            high_ref[x - (SLAB - HALO)] = short
+            head = jnp.concatenate([sent[0][:BATCH], extra.astype(BF16)], axis=0)
+            sent = [head, sent[0][BATCH:]]
+        for k, short in enumerate(sent):
+            if x < HALO:
+                halos[2 * k][x] = short
+            if x >= SLAB - HALO:
+                halos[2 * k + 1][x - (SLAB - HALO)] = short
 
 
 def project(line, full, others, field, core_x, local):
     rows = field.shape[1]
-    sent = rows + (EXTRA if local is not None else 0)
+    sizes = [rows] if local is None else [BATCH + EXTRA, rows - BATCH]
     return line.call(
         project_kernel,
-        (
-            struct((SLAB, rows, PLANE), F32),
-            struct((HALO, sent, PLANE), BF16),
-            struct((HALO, sent, PLANE), BF16),
-        ),
+        (struct((SLAB, rows, PLANE), F32),)
+        + tuple(struct((HALO, n, PLANE), BF16) for n in sizes for _ in range(2)),
         (full, *others, field, core_x) + ((local,) if local is not None else ()),
         micros=2,
     )
@@ -306,7 +306,7 @@
         weight_ref, first_ref, flag_ref, core_ref = refs[3:7]
         others, (out_ref, full_ref, half_ref) = refs[7:-7], refs[-7:-4]
     below, above, even, odd = refs[-4:]
-    rows = field_ref.shape[1]
+    rows = BATCH
     if mode == "first":
         weight_ref[HALO : HALO + SLAB] = 8.0 * local_ref[...] - 2.0
         for k, ref in enumerate((below_ref, above_ref)):
@@ -375,7 +375,7 @@
 
     @pl.loop(0, out_ref.shape[1] // 16)
     def _(i):
-        both = pl.ds(pl.multiple_of(offset + i * 16, 16), 16)
+        both = pl.ds(pl.multiple_of(i * 16, 16), 16)
         below[...] = below_ref[:, both, :].astype(F32)
         above[...] = above_ref[:, both, :].astype(F32)
 
@@ -489,17 +489,19 @@
     second = permute_groups(mate, [(i, (i + 2) % groups) for i in range(0, groups, 2)])
     mapped, full, half = map_batches(line, pick, core_x, [(stochastic,), (third,)])
     others = exchange(half)
-    field, low, high = project(line, full, others, mapped, core_x, local)
+    field, low, high, low_more, high_more = project(line, full, others, mapped, core_x, local)
     below = lax.ppermute(high, "grid", UP)
     above = lax.ppermute(low, "grid", DOWN)
 
     mapped_rest, full, half = map_batches(line, pick, core_x, [(mate, second)])
     others = exchange(half)
+    below_more = lax.ppermute(high_more, "grid", UP)
+    above_more = lax.ppermute(low_more, "grid", DOWN)
     weight, first = filter_first(line, field, below, above, local)
     rest, low, high = project(line, full, others, mapped_rest, core_x, None)
     below_rest = lax.ppermute(high, "grid", UP)
     above_rest = lax.ppermute(low, "grid", DOWN)
-    more = filter_more(line, field, below, above, weight)
+    more = filter_more(line, field, below_more, above_more, weight)
     last, full, half = filter_last(
         line, rest, below_rest, above_rest, weight, core_x, (first, more)
     )

time: 100 us -> 90.1 us (0.901)
  waiting for transfers between devices: 31.8 us -> 18.5 us
  starting transfers between devices: 24 us -> 27.6 us
    ppermute x3, waiting for transfers between devices: 24.4 us -> 12.9 us  [permute_groups(): return lax.ppermute(array, 'group', pairs)]
    ppermute x0 -> x2, starting transfers between devices: none -> 5.04 us  [the longest x1 3.75 us: body(): below_more = lax.ppermute(high_more, 'grid', UP)]
    ppermute x9, waiting for transfers between devices: 7.42 us -> 5.49 us  [exchange(): lax.ppermute(half, 'grid', [(i, i ^ k) for i in range(GRID)])]
  transfers between devices with their start and end apart: 16 -> 18, of which waited for: 6 -> 5; matrix products, arithmetic and copies ran while one was open for 0% -> 0% of each run, Pallas kernels for 23% -> 29%
where the time goes in v2:
time: 90.1 us; the launch traced here: 89.9 us
  Pallas kernels  43 us (48%)
  starting transfers between devices  27.6 us (31%)
  waiting for transfers between devices  18.5 us (21%)
    pallas_call x10, Pallas kernels, call(): pl.pallas_call(with_token, in_specs=specs, out_specs=tuple((VMEM for _ in...  43 us
    ppermute x3, waiting for transfers between devices, permute_groups(): return lax.ppermute(array, 'group', pairs)  12.9 us
    ppermute x9, starting transfers between devices, exchange(): lax.ppermute(half, 'grid', [(i, i ^ k) for i in range(GRID)])  8.76 us
    ppermute x3, starting transfers between devices, permute_groups(): return lax.ppermute(array, 'group', pairs)  7.21 us
    ppermute x9, waiting for transfers between devices, exchange(): lax.ppermute(half, 'grid', [(i, i ^ k) for i in range(GRID)])  5.49 us
    ppermute x1, starting transfers between devices, body(): below_more = lax.ppermute(high_more, 'grid', UP)  3.75 us
    ppermute x1, starting transfers between devices, body(): below = lax.ppermute(high, 'grid', UP)  2.05 us
    ppermute x1, starting transfers between devices, body(): below_rest = lax.ppermute(high, 'grid', UP)  1.93 us
  transfers between devices with their start and end apart: 18, of which 5 were waited for; matrix products, arithmetic and copies ran while one was open for 0% of the time, Pallas kernels for 29%

profile of v2, /device:TPU:0, one launch (start us, length us, event | category | flops | bytes accessed | tf_op | source)
XLA Modules:
  0.0 89.9 jit_solution(11695736456609302323)
XLA Ops:
  0.6 3.4 %collective-permute-start = (bf16[32,8,1024]{2,1,0:T(8,128)(2,1)}, bf16[32,8,1024]{2,1,0:T(8,128)(2,1)S(1)}, u32[]{:S(2)}, u32[]{:S(2)}) collective-permute-start(bf16[32,8,1024]{2,1,0:T(8,128)(2,1)} %param.4), channel_id=1, source_target_pairs={{0,4},{4,0},{8,12},{12,8},{16,20},{20,16},{24,28},{28,24},{32,36},... | collective-permute-start | bytes 1572872 | tf_op jit(solution)/shard_map/ppermute | solution.py:476
  4.0 1.9 %collective-permute-start.2 = (bf16[32,8,1024]{2,1,0:T(8,128)(2,1)}, bf16[32,8,1024]{2,1,0:T(8,128)(2,1)S(1)}, u32[]{:S(2)}, u32[]{:S(2)}) collective-permute-start(bf16[32,8,1024]{2,1,0:T(8,128)(2,1)} %param.4), channel_id=1, source_target_pairs={{0,8},{4,12},{8,16},{12,20},{16,24},{20,28},{24,32},{28,36},{32,40... | collective-permute-start | bytes 1572872 | tf_op jit(solution)/shard_map/ppermute | solution.py:476
  5.9 0.0 copy-start.1
  5.9 0.0 copy-start.2
  5.9 7.2 %shard_map.59 = (bf16[8,512,1024]{2,1,0:T(8,128)(2,1)S(1)}, f32[8,128]{1,0:T(8,128)S(1)}) custom-call(bf16[4096,1024]{1,0:T(8,128)(2,1)} %bitcast.13), custom_call_target="tpu_custom_call" | custom-call | flops 4000000000 | bytes 1024 | tf_op jit(solution)/shard_map/pallas_call | solution.py:74
  13.1 0.0 copy-start
  13.2 0.0 copy-done.1
  13.2 0.0 copy-done.2
  13.2 1.8 %shard_map.60 = (bf16[1024,1024]{1,0:T(8,128)(2,1)S(1)}, bf16[1024,1024]{1,0:T(8,128)(2,1)S(1)}, f32[8,1024]{1,0:T(8,128)S(1)}, f32[8,128]{1,0:T(8,128)S(1)}) custom-call(s32[1,1024]{1,0:T(1,128)S(1)} %copy-done.2, f32[8,1024]{1,0:T(8,128)S(1)} %bitcast.12, f32[8,128]{1,0:T(8,128)S(1)} %get-tuple-element.41.refs_2_), custom_call_target="tpu_custom_call" | custom-call | flops 1000000000 | bytes 1024 | tf_op jit(solution)/shard_map/pallas_call | solution.py:74
  15.0 1.1 %collective-permute-done = bf16[32,8,1024]{2,1,0:T(8,128)(2,1)S(1)} collective-permute-done((bf16[32,8,1024]{2,1,0:T(8,128)(2,1)}, bf16[32,8,1024]{2,1,0:T(8,128)(2,1)S(1)}, u32[]{:S(2)}, u32[]{:S(2)}) %collective-permute-start) | collective-permute-done | bytes 524320 | tf_op jit(solution)/shard_map/ppermute | solution.py:476
  16.2 6.0 %collective-permute-done.2 = bf16[32,8,1024]{2,1,0:T(8,128)(2,1)S(1)} collective-permute-done((bf16[32,8,1024]{2,1,0:T(8,128)(2,1)}, bf16[32,8,1024]{2,1,0:T(8,128)(2,1)S(1)}, u32[]{:S(2)}, u32[]{:S(2)}) %collective-permute-start.2) | collective-permute-done | bytes 524320 | tf_op jit(solution)/shard_map/ppermute | solution.py:476
  22.1 0.0 copy-done
  22.1 4.0 %shard_map.61 = (bf16[8,64,1024]{2,1,0:T(8,128)(2,1)S(1)}, f32[64,512]{1,0:T(8,128)S(1)}, bf16[64,512]{1,0:T(8,128)(2,1)S(1)}, f32[8,128]{1,0:T(8,128)S(1)}) custom-call(bf16[1024,1024]{1,0:T(8,128)(2,1)S(1)} %get-tuple-element.42.refs_0_, bf16[8,512,1024]{2,1,0:T(8,128)(2,1)S(1)} %get-tuple-element.43.refs_1_.refs_5_.refs_6_.refs_9_, ...), custom_call_target="tpu_custom_call" | custom-call | flops 1500000000 | bytes 1024 | tf_op jit(solution)/shard_map/pallas_call | solution.py:74
  26.2 0.1 collective-permute-start.5
  26.3 0.8 collective-permute-start.4
  27.0 1.1 %collective-permute-start.3 = (bf16[64,512]{1,0:T(8,128)(2,1)S(1)}, bf16[64,512]{1,0:T(8,128)(2,1)S(1)}, u32[]{:S(2)}, u32[]{:S(2)}) collective-permute-start(bf16[64,512]{1,0:T(8,128)(2,1)S(1)} %get-tuple-element.48), channel_id=1, source_target_pairs={{0,1},{1,0},{2,3},{3,2},{4,5},{5,4},{6,7},{7,6},{8,9},{9,8},{10,11... | collective-permute-start | bytes 196616 | tf_op jit(solution)/shard_map/ppermute | solution.py:251
  28.1 1.9 %collective-permute-start.1 = (bf16[32,8,1024]{2,1,0:T(8,128)(2,1)S(1)}, bf16[32,8,1024]{2,1,0:T(8,128)(2,1)S(1)}, u32[]{:S(2)}, u32[]{:S(2)}) collective-permute-start(bf16[32,8,1024]{2,1,0:T(8,128)(2,1)S(1)} %collective-permute-done), channel_id=1, source_target_pairs={{0,8},{8,16},{16,24},{24,32},{32,40},{40,48},{48,56},{56,64},{64,7... | collective-permute-start | bytes 1572872 | tf_op jit(solution)/shard_map/ppermute | solution.py:476
  30.0 0.0 collective-permute-done.5.refs_3_
  30.0 1.3 %collective-permute-done.4.refs_2_ = bf16[64,512]{1,0:T(8,128)(2,1)S(1)} collective-permute-done((bf16[64,512]{1,0:T(8,128)(2,1)S(1)}, bf16[64,512]{1,0:T(8,128)(2,1)S(1)}, u32[]{:S(2)}, u32[]{:S(2)}) %collective-permute-start.4) | collective-permute-done | bytes 65568 | tf_op jit(solution)/shard_map/ppermute | solution.py:251
  31.3 0.0 collective-permute-done.3.refs_1_
  31.3 1.6 %shard_map.62 = (f32[8,64,1024]{2,1,0:T(8,128)S(1)}, bf16[6,40,1024]{2,1,0:T(8,128)(2,1)S(1)}, bf16[6,40,1024]{2,1,0:T(8,128)(2,1)S(1)}, bf16[6,32,1024]{2,1,0:T...) custom-call(f32[64,512]{1,0:T(8,128)S(1)} %get-tuple-element.47.refs_0_, ...), custom_call_target="tpu_custom_call" | custom-call | flops 1000000000 | bytes 1024 | tf_op jit(solution)/shard_map/pallas_call | solution.py:74
  32.9 2.0 %collective-permute-start.9 = (bf16[6,40,1024]{2,1,0:T(8,128)(2,1)S(1)}, bf16[6,40,1024]{2,1,0:T(8,128)(2,1)S(1)}, u32[]{:S(2)}, u32[]{:S(2)}) collective-permute-start(bf16[6,40,1024]{2,1,0:T(8,128)(2,1)S(1)} %get-tuple-element.57), channel_id=1, source_target_pairs={{0,1},{1,2},{2,3},{4,5},{5,6},{6,7},{8,9},{9,10},{10,11},{12,13},{... | collective-permute-start | bytes 1474568 | tf_op jit(solution)/shard_map/ppermute | solution.py:493
  35.0 1.3 %collective-permute-start.10 = (bf16[6,40,1024]{2,1,0:T(8,128)(2,1)S(1)}, bf16[6,40,1024]{2,1,0:T(8,128)(2,1)S(1)}, u32[]{:S(2)}, u32[]{:S(2)}) collective-permute-start(bf16[6,40,1024]{2,1,0:T(8,128)(2,1)S(1)} %get-tuple-element.58), channel_id=1, source_target_pairs={{1,0},{2,1},{3,2},{5,4},{6,5},{7,6},{9,8},{10,9},{11,10},{13,12},{... | collective-permute-start | bytes 1474568 | tf_op jit(solution)/shard_map/ppermute | solution.py:494
  36.3 3.7 %collective-permute-start.13 = (bf16[6,32,1024]{2,1,0:T(8,128)(2,1)S(1)}, bf16[6,32,1024]{2,1,0:T(8,128)(2,1)S(1)}, u32[]{:S(2)}, u32[]{:S(2)}) collective-permute-start(bf16[6,32,1024]{2,1,0:T(8,128)(2,1)S(1)} %get-tuple-element.68), channel_id=1, source_target_pairs={{0,1},{1,2},{2,3},{4,5},{5,6},{6,7},{8,9},{9,10},{10,11},{12,13},{... | collective-permute-start | bytes 1179656 | tf_op jit(solution)/shard_map/ppermute | solution.py:498
  40.0 1.3 %collective-permute-start.14 = (bf16[6,32,1024]{2,1,0:T(8,128)(2,1)S(1)}, bf16[6,32,1024]{2,1,0:T(8,128)(2,1)S(1)}, u32[]{:S(2)}, u32[]{:S(2)}) collective-permute-start(bf16[6,32,1024]{2,1,0:T(8,128)(2,1)S(1)} %get-tuple-element.69), channel_id=1, source_target_pairs={{1,0},{2,1},{3,2},{5,4},{6,5},{7,6},{9,8},{10,9},{11,10},{13,12},{... | collective-permute-start | bytes 1179656 | tf_op jit(solution)/shard_map/ppermute | solution.py:499
  41.3 5.8 %collective-permute-done.1 = bf16[32,8,1024]{2,1,0:T(8,128)(2,1)S(1)} collective-permute-done((bf16[32,8,1024]{2,1,0:T(8,128)(2,1)S(1)}, bf16[32,8,1024]{2,1,0:T(8,128)(2,1)S(1)}, u32[]{:S(2)}, u32[]{:S(2)}) %collective-permute-start.1) | collective-permute-done | bytes 524320 | tf_op jit(solution)/shard_map/ppermute | solution.py:476
  47.2 3.3 %shard_map.63 = (bf16[8,32,1024]{2,1,0:T(8,128)(2,1)S(1)}, f32[32,512]{1,0:T(8,128)S(1)}, bf16[32,512]{1,0:T(8,128)(2,1)S(1)}, f32[8,128]{1,0:T(8,128)S(1)}) custom-call(bf16[1024,1024]{1,0:T(8,128)(2,1)S(1)} %get-tuple-element.42.refs_0_, bf16[8,512,1024]{2,1,0:T(8,128)(2,1)S(1)} %get-tuple-element.43.refs_1_.refs_5_.refs_6_.refs_9_, ...), custom_call_target="tpu_custom_call" | custom-call | flops 1000000000 | bytes 1024 | tf_op jit(solution)/shard_map/pallas_call | solution.py:74
  50.4 0.0 collective-permute-start.8
  50.5 0.0 collective-permute-done.9.refs_1_
  50.5 0.8 collective-permute-start.7
  51.3 0.0 collective-permute-done.10.refs_2_
  51.3 1.0 %collective-permute-start.6 = (bf16[32,512]{1,0:T(8,128)(2,1)S(1)}, bf16[32,512]{1,0:T(8,128)(2,1)S(1)}, u32[]{:S(2)}, u32[]{:S(2)}) collective-permute-start(bf16[32,512]{1,0:T(8,128)(2,1)S(1)} %get-tuple-element.54), channel_id=1, source_target_pairs={{0,1},{1,0},{2,3},{3,2},{4,5},{5,4},{6,7},{7,6},{8,9},{9,8},{10,11... | collective-permute-start | bytes 98312 | tf_op jit(solution)/shard_map/ppermute | solution.py:251
  52.3 5.5 %shard_map.64 = (f32[20,1024]{1,0:T(8,128)S(1)}, f32[20,1024]{1,0:T(8,128)S(1)}, f32[2,8,128]{2,1,0:T(8,128)S(1)}, f32[8,32,1024]{2,1,0:T(8,128)S(1)}, f32[8,128]{1,0:T(8,128)S(1)}) custom-call(f32[8,64,1024]{2,1,0:T(8,128)S(1)} %get-tuple-element.56.refs_0_, bf16[6,40,1024]{2,1,0:T(8,128)(2,1)S(1)} %collective-permute-done.9.refs_1_, ...), custom_call_target="tpu_custom_call" | custom-call | flops 3000000000 | bytes 1024 | tf_op jit(solution)/shard_map/pallas_call | solution.py:74
  57.8 0.0 collective-permute-done.8.refs_3_
  57.8 0.0 collective-permute-done.7.refs_2_
  57.8 0.0 collective-permute-done.6.refs_1_
  57.9 1.6 %shard_map.65 = (f32[8,32,1024]{2,1,0:T(8,128)S(1)}, bf16[6,32,1024]{2,1,0:T(8,128)(2,1)S(1)}, bf16[6,32,1024]{2,1,0:T(8,128)(2,1)S(1)}, f32[8,128]{1,0:T(8,128)S(1)}) custom-call(f32[32,512]{1,0:T(8,128)S(1)} %get-tuple-element.53.refs_0_, bf16[32,512]{1,0:T(8,128)(2,1)S(1)} %collective-permute-done.6.refs_1_, ...), custom_call_target="tpu_custom_call" | custom-call | flops 1000000000 | bytes 1024 | tf_op jit(solution)/shard_map/pallas_call | solution.py:74
  59.4 1.9 %collective-permute-start.11 = (bf16[6,32,1024]{2,1,0:T(8,128)(2,1)S(1)}, bf16[6,32,1024]{2,1,0:T(8,128)(2,1)S(1)}, u32[]{:S(2)}, u32[]{:S(2)}) collective-permute-start(bf16[6,32,1024]{2,1,0:T(8,128)(2,1)S(1)} %get-tuple-element.62), channel_id=1, source_target_pairs={{0,1},{1,2},{2,3},{4,5},{5,6},{6,7},{8,9},{9,10},{10,11},{12,13},{... | collective-permute-start | bytes 1179656 | tf_op jit(solution)/shard_map/ppermute | solution.py:502
  61.3 1.3 %collective-permute-start.12 = (bf16[6,32,1024]{2,1,0:T(8,128)(2,1)S(1)}, bf16[6,32,1024]{2,1,0:T(8,128)(2,1)S(1)}, u32[]{:S(2)}, u32[]{:S(2)}) collective-permute-start(bf16[6,32,1024]{2,1,0:T(8,128)(2,1)S(1)} %get-tuple-element.63), channel_id=1, source_target_pairs={{1,0},{2,1},{3,2},{5,4},{6,5},{7,6},{9,8},{10,9},{11,10},{13,12},{... | collective-permute-start | bytes 1179656 | tf_op jit(solution)/shard_map/ppermute | solution.py:503
  62.6 0.0 collective-permute-done.13.refs_1_
  62.7 0.0 collective-permute-done.14.refs_2_
  62.7 5.4 %shard_map.66 = (f32[8,32,1024]{2,1,0:T(8,128)S(1)}, f32[8,128]{1,0:T(8,128)S(1)}) custom-call(f32[8,64,1024]{2,1,0:T(8,128)S(1)} %get-tuple-element.56.refs_0_, bf16[6,32,1024]{2,1,0:T(8,128)(2,1)S(1)} %collective-permute-done.13.refs_1_, bf16[6,32,1024]{2,1,0:T(8,128)(2,1)S(1)} %collective-permute-done.14.refs_2_, ...), custom_call_target="tpu_custom_call" | custom-call | flops 3000000000 | bytes 1024 | tf_op jit(solution)/shard_map/pallas_call | solution.py:74
  68.0 0.0 collective-permute-done.11.refs_1_
  68.1 0.0 collective-permute-done.12.refs_2_
  68.1 8.3 %shard_map.67 = (f32[8,32,1024]{2,1,0:T(8,128)S(1)}, f32[96,512]{1,0:T(8,128)S(1)}, bf16[96,512]{1,0:T(8,128)(2,1)S(1)}, f32[8,128]{1,0:T(8,128)S(1)}) custom-call(f32[8,32,1024]{2,1,0:T(8,128)S(1)} %get-tuple-element.61.refs_0_, bf16[6,32,1024]{2,1,0:T(8,128)(2,1)S(1)} %collective-permute-done.11.refs_1_, ...), custom_call_target="tpu_custom_call" | custom-call | flops 4000000000 | bytes 1024 | tf_op jit(solution)/shard_map/pallas_call | solution.py:74
  76.4 1.6 %collective-permute-start.17 = (bf16[96,512]{1,0:T(8,128)(2,1)S(1)}, bf16[96,512]{1,0:T(8,128)(2,1)S(1)}, u32[]{:S(2)}, u32[]{:S(2)}) collective-permute-start(bf16[96,512]{1,0:T(8,128)(2,1)S(1)} %get-tuple-element.74), channel_id=1, source_target_pairs={{0,3},{1,2},{2,1},{3,0},{4,7},{5,6},{6,5},{7,4},{8,11},{9,10},{10,... | collective-permute-start | bytes 294920 | tf_op jit(solution)/shard_map/ppermute | solution.py:251
  78.0 3.4 %collective-permute-start.16 = (bf16[96,512]{1,0:T(8,128)(2,1)S(1)}, bf16[96,512]{1,0:T(8,128)(2,1)S(1)}, u32[]{:S(2)}, u32[]{:S(2)}) collective-permute-start(bf16[96,512]{1,0:T(8,128)(2,1)S(1)} %get-tuple-element.74), channel_id=1, source_target_pairs={{0,2},{1,3},{2,0},{3,1},{4,6},{5,7},{6,4},{7,5},{8,10},{9,11},{10,... | collective-permute-start | bytes 294920 | tf_op jit(solution)/shard_map/ppermute | solution.py:251
  81.4 0.0 collective-permute-start.15
  81.4 0.0 collective-permute-done.17.refs_3_
  81.4 4.2 %collective-permute-done.16.refs_2_ = bf16[96,512]{1,0:T(8,128)(2,1)S(1)} collective-permute-done((bf16[96,512]{1,0:T(8,128)(2,1)S(1)}, bf16[96,512]{1,0:T(8,128)(2,1)S(1)}, u32[]{:S(2)}, u32[]{:S(2)}) %collective-permute-start.16) | collective-permute-done | bytes 98336 | tf_op jit(solution)/shard_map/ppermute | solution.py:251
  85.6 0.0 collective-permute-done.15.refs_1_
  85.6 4.3 %shard_map.68 = (f32[256,1024]{1,0:T(8,128)}, f32[8,1024]{1,0:T(8,128)}, f32[8,128]{1,0:T(8,128)}) custom-call(f32[96,512]{1,0:T(8,128)S(1)} %get-tuple-element.73.refs_0_, bf16[96,512]{1,0:T(8,128)(2,1)S(1)} %collective-permute-done.15.refs_1_, bf16[96,512]{1,0:T(8,128)(2,1)S(1)} %collective-permute-done.16.refs_2_, ...), custom_call_target="tpu_custom_call" | custom-call | flops 2000000000 | bytes 1024 | tf_op jit(solution)/shard_map/pallas_call | solution.py:74
Async XLA Ops:
  0.6 15.5 %collective-permute-start = (bf16[32,8,1024]{2,1,0:T(8,128)(2,1)}, bf16[32,8,1024]{2,1,0:T(8,128)(2,1)S(1)}, u32[]{:S(2)}, u32[]{:S(2)}) collective-permute-start(bf16[32,8,1024]{2,1,0:T(8,128)(2,1)} %param.4), channel_id=1, source_target_pairs={{0,4},{4,0},{8,12},{12,8},{16,20},{20,16},{24,28},{28,24},{32,36},... | collective-permute-start | bytes 1572872 | tf_op jit(solution)/shard_map/ppermute | solution.py:476
  4.0 18.1 %collective-permute-start.2 = (bf16[32,8,1024]{2,1,0:T(8,128)(2,1)}, bf16[32,8,1024]{2,1,0:T(8,128)(2,1)S(1)}, u32[]{:S(2)}, u32[]{:S(2)}) collective-permute-start(bf16[32,8,1024]{2,1,0:T(8,128)(2,1)} %param.4), channel_id=1, source_target_pairs={{0,8},{4,12},{8,16},{12,20},{16,24},{20,28},{24,32},{28,36},{32,40... | collective-permute-start | bytes 1572872 | tf_op jit(solution)/shard_map/ppermute | solution.py:476
  5.9 7.2 %copy-start.1 = (f32[1,8,1024]{2,1,0:T(8,128)S(1)}, f32[1,8,1024]{2,1,0:T(8,128)}, u32[]{:S(2)}) copy-start(f32[1,8,1024]{2,1,0:T(8,128)} %param.7) | copy-start | bytes 98308
  5.9 7.2 %copy-start.2 = (s32[1,1024]{1,0:T(1,128)S(1)}, s32[1,1024]{1,0:T(1,128)}, u32[]{:S(2)}) copy-start(s32[1,1024]{1,0:T(1,128)} %refs_0_.1) | copy-start | bytes 12292
  13.1 9.0 %copy-start = (bf16[32,8,1024]{2,1,0:T(8,128)(2,1)S(1)}, bf16[32,8,1024]{2,1,0:T(8,128)(2,1)}, u32[]{:S(2)}) copy-start(bf16[32,8,1024]{2,1,0:T(8,128)(2,1)} %param.4) | copy-start | bytes 1572868
  26.2 3.9 %collective-permute-start.5 = (bf16[64,512]{1,0:T(8,128)(2,1)S(1)}, bf16[64,512]{1,0:T(8,128)(2,1)S(1)}, u32[]{:S(2)}, u32[]{:S(2)}) collective-permute-start(bf16[64,512]{1,0:T(8,128)(2,1)S(1)} %get-tuple-element.48), channel_id=1, source_target_pairs={{0,3},{1,2},{2,1},{3,0},{4,7},{5,6},{6,5},{7,4},{8,11},{9,10},{10,... | collective-permute-start | bytes 196616 | tf_op jit(solution)/shard_map/ppermute | solution.py:251
  26.3 5.0 %collective-permute-start.4 = (bf16[64,512]{1,0:T(8,128)(2,1)S(1)}, bf16[64,512]{1,0:T(8,128)(2,1)S(1)}, u32[]{:S(2)}, u32[]{:S(2)}) collective-permute-start(bf16[64,512]{1,0:T(8,128)(2,1)S(1)} %get-tuple-element.48), channel_id=1, source_target_pairs={{0,2},{1,3},{2,0},{3,1},{4,6},{5,7},{6,4},{7,5},{8,10},{9,11},{10,... | collective-permute-start | bytes 196616 | tf_op jit(solution)/shard_map/ppermute | solution.py:251
  27.0 4.3 %collective-permute-start.3 = (bf16[64,512]{1,0:T(8,128)(2,1)S(1)}, bf16[64,512]{1,0:T(8,128)(2,1)S(1)}, u32[]{:S(2)}, u32[]{:S(2)}) collective-permute-start(bf16[64,512]{1,0:T(8,128)(2,1)S(1)} %get-tuple-element.48), channel_id=1, source_target_pairs={{0,1},{1,0},{2,3},{3,2},{4,5},{5,4},{6,7},{7,6},{8,9},{9,8},{10,11... | collective-permute-start | bytes 196616 | tf_op jit(solution)/shard_map/ppermute | solution.py:251
  28.1 19.0 %collective-permute-start.1 = (bf16[32,8,1024]{2,1,0:T(8,128)(2,1)S(1)}, bf16[32,8,1024]{2,1,0:T(8,128)(2,1)S(1)}, u32[]{:S(2)}, u32[]{:S(2)}) collective-permute-start(bf16[32,8,1024]{2,1,0:T(8,128)(2,1)S(1)} %collective-permute-done), channel_id=1, source_target_pairs={{0,8},{8,16},{16,24},{24,32},{32,40},{40,48},{48,56},{56,64},{64,7... | collective-permute-start | bytes 1572872 | tf_op jit(solution)/shard_map/ppermute | solution.py:476
  32.9 17.5 %collective-permute-start.9 = (bf16[6,40,1024]{2,1,0:T(8,128)(2,1)S(1)}, bf16[6,40,1024]{2,1,0:T(8,128)(2,1)S(1)}, u32[]{:S(2)}, u32[]{:S(2)}) collective-permute-start(bf16[6,40,1024]{2,1,0:T(8,128)(2,1)S(1)} %get-tuple-element.57), channel_id=1, source_target_pairs={{0,1},{1,2},{2,3},{4,5},{5,6},{6,7},{8,9},{9,10},{10,11},{12,13},{... | collective-permute-start | bytes 1474568 | tf_op jit(solution)/shard_map/ppermute | solution.py:493
  35.0 16.3 %collective-permute-start.10 = (bf16[6,40,1024]{2,1,0:T(8,128)(2,1)S(1)}, bf16[6,40,1024]{2,1,0:T(8,128)(2,1)S(1)}, u32[]{:S(2)}, u32[]{:S(2)}) collective-permute-start(bf16[6,40,1024]{2,1,0:T(8,128)(2,1)S(1)} %get-tuple-element.58), channel_id=1, source_target_pairs={{1,0},{2,1},{3,2},{5,4},{6,5},{7,6},{9,8},{10,9},{11,10},{13,12},{... | collective-permute-start | bytes 1474568 | tf_op jit(solution)/shard_map/ppermute | solution.py:494
  36.3 26.4 %collective-permute-start.13 = (bf16[6,32,1024]{2,1,0:T(8,128)(2,1)S(1)}, bf16[6,32,1024]{2,1,0:T(8,128)(2,1)S(1)}, u32[]{:S(2)}, u32[]{:S(2)}) collective-permute-start(bf16[6,32,1024]{2,1,0:T(8,128)(2,1)S(1)} %get-tuple-element.68), channel_id=1, source_target_pairs={{0,1},{1,2},{2,3},{4,5},{5,6},{6,7},{8,9},{9,10},{10,11},{12,13},{... | collective-permute-start | bytes 1179656 | tf_op jit(solution)/shard_map/ppermute | solution.py:498
  40.0 22.6 %collective-permute-start.14 = (bf16[6,32,1024]{2,1,0:T(8,128)(2,1)S(1)}, bf16[6,32,1024]{2,1,0:T(8,128)(2,1)S(1)}, u32[]{:S(2)}, u32[]{:S(2)}) collective-permute-start(bf16[6,32,1024]{2,1,0:T(8,128)(2,1)S(1)} %get-tuple-element.69), channel_id=1, source_target_pairs={{1,0},{2,1},{3,2},{5,4},{6,5},{7,6},{9,8},{10,9},{11,10},{13,12},{... | collective-permute-start | bytes 1179656 | tf_op jit(solution)/shard_map/ppermute | solution.py:499
  50.4 7.4 %collective-permute-start.8 = (bf16[32,512]{1,0:T(8,128)(2,1)S(1)}, bf16[32,512]{1,0:T(8,128)(2,1)S(1)}, u32[]{:S(2)}, u32[]{:S(2)}) collective-permute-start(bf16[32,512]{1,0:T(8,128)(2,1)S(1)} %get-tuple-element.54), channel_id=1, source_target_pairs={{0,3},{1,2},{2,1},{3,0},{4,7},{5,6},{6,5},{7,4},{8,11},{9,10},{10,... | collective-permute-start | bytes 98312 | tf_op jit(solution)/shard_map/ppermute | solution.py:251
  50.5 7.4 %collective-permute-start.7 = (bf16[32,512]{1,0:T(8,128)(2,1)S(1)}, bf16[32,512]{1,0:T(8,128)(2,1)S(1)}, u32[]{:S(2)}, u32[]{:S(2)}) collective-permute-start(bf16[32,512]{1,0:T(8,128)(2,1)S(1)} %get-tuple-element.54), channel_id=1, source_target_pairs={{0,2},{1,3},{2,0},{3,1},{4,6},{5,7},{6,4},{7,5},{8,10},{9,11},{10,... | collective-permute-start | bytes 98312 | tf_op jit(solution)/shard_map/ppermute | solution.py:251
  51.3 6.5 %collective-permute-start.6 = (bf16[32,512]{1,0:T(8,128)(2,1)S(1)}, bf16[32,512]{1,0:T(8,128)(2,1)S(1)}, u32[]{:S(2)}, u32[]{:S(2)}) collective-permute-start(bf16[32,512]{1,0:T(8,128)(2,1)S(1)} %get-tuple-element.54), channel_id=1, source_target_pairs={{0,1},{1,0},{2,3},{3,2},{4,5},{5,4},{6,7},{7,6},{8,9},{9,8},{10,11... | collective-permute-start | bytes 98312 | tf_op jit(solution)/shard_map/ppermute | solution.py:251
  59.4 8.6 %collective-permute-start.11 = (bf16[6,32,1024]{2,1,0:T(8,128)(2,1)S(1)}, bf16[6,32,1024]{2,1,0:T(8,128)(2,1)S(1)}, u32[]{:S(2)}, u32[]{:S(2)}) collective-permute-start(bf16[6,32,1024]{2,1,0:T(8,128)(2,1)S(1)} %get-tuple-element.62), channel_id=1, source_target_pairs={{0,1},{1,2},{2,3},{4,5},{5,6},{6,7},{8,9},{9,10},{10,11},{12,13},{... | collective-permute-start | bytes 1179656 | tf_op jit(solution)/shard_map/ppermute | solution.py:502
  61.3 6.7 %collective-permute-start.12 = (bf16[6,32,1024]{2,1,0:T(8,128)(2,1)S(1)}, bf16[6,32,1024]{2,1,0:T(8,128)(2,1)S(1)}, u32[]{:S(2)}, u32[]{:S(2)}) collective-permute-start(bf16[6,32,1024]{2,1,0:T(8,128)(2,1)S(1)} %get-tuple-element.63), channel_id=1, source_target_pairs={{1,0},{2,1},{3,2},{5,4},{6,5},{7,6},{9,8},{10,9},{11,10},{13,12},{... | collective-permute-start | bytes 1179656 | tf_op jit(solution)/shard_map/ppermute | solution.py:503
  76.4 4.9 %collective-permute-start.17 = (bf16[96,512]{1,0:T(8,128)(2,1)S(1)}, bf16[96,512]{1,0:T(8,128)(2,1)S(1)}, u32[]{:S(2)}, u32[]{:S(2)}) collective-permute-start(bf16[96,512]{1,0:T(8,128)(2,1)S(1)} %get-tuple-element.74), channel_id=1, source_target_pairs={{0,3},{1,2},{2,1},{3,0},{4,7},{5,6},{6,5},{7,4},{8,11},{9,10},{10,... | collective-permute-start | bytes 294920 | tf_op jit(solution)/shard_map/ppermute | solution.py:251
  78.0 7.6 %collective-permute-start.16 = (bf16[96,512]{1,0:T(8,128)(2,1)S(1)}, bf16[96,512]{1,0:T(8,128)(2,1)S(1)}, u32[]{:S(2)}, u32[]{:S(2)}) collective-permute-start(bf16[96,512]{1,0:T(8,128)(2,1)S(1)} %get-tuple-element.74), channel_id=1, source_target_pairs={{0,2},{1,3},{2,0},{3,1},{4,6},{5,7},{6,4},{7,5},{8,10},{9,11},{10,... | collective-permute-start | bytes 294920 | tf_op jit(solution)/shard_map/ppermute | solution.py:251
  81.4 4.2 %collective-permute-start.15 = (bf16[96,512]{1,0:T(8,128)(2,1)S(1)}, bf16[96,512]{1,0:T(8,128)(2,1)S(1)}, u32[]{:S(2)}, u32[]{:S(2)}) collective-permute-start(bf16[96,512]{1,0:T(8,128)(2,1)S(1)} %get-tuple-element.74), channel_id=1, source_target_pairs={{0,1},{1,0},{2,3},{3,2},{4,5},{5,4},{6,7},{7,6},{8,9},{9,8},{10,11... | collective-permute-start | bytes 294920 | tf_op jit(solution)/shard_map/ppermute | solution.py:251

commit v3 on v0

--- a/solution.py
+++ b/solution.py
@@ -47,6 +47,7 @@
 MIB = 1 << 20
 PIECE = 32
 SCALE = 500e6
+EXTRA = 8
 CHUNKS = NCORE // PIECE
 NT = (((1,), (1,)), ((), ()))
 
@@ -266,7 +267,7 @@
         short = value.astype(BF16)
         if local_ref is not None:
             parts = [p.astype(F32) for p in split(local_ref[x : x + 1], 3)]
-            rest = jnp.zeros((12, PLANE), F32)
+            rest = jnp.zeros((EXTRA - 4, PLANE), F32)
             extra = jnp.concatenate(parts + [jnp.ones((1, PLANE), F32), rest], axis=0)
             short = jnp.concatenate([short, extra.astype(BF16)], axis=0)
         if x < HALO:
@@ -277,7 +278,7 @@
 
 def project(line, full, others, field, core_x, local):
     rows = field.shape[1]
-    sent = rows + (16 if local is not None else 0)
+    sent = rows + (EXTRA if local is not None else 0)
     return line.call(
         project_kernel,
         (
@@ -306,7 +307,7 @@
         weight_ref[HALO : HALO + SLAB] = 8.0 * local_ref[...] - 2.0
         for k, ref in enumerate((below_ref, above_ref)):
             for x in range(HALO):
-                extra = ref[x, rows : rows + 16, :].astype(F32)
+                extra = ref[x, rows : rows + EXTRA, :].astype(F32)
                 near = (extra[0:1] + extra[1:2]) + extra[2:3]
                 place = x if k == 0 else HALO + SLAB + x
                 weight_ref[place : place + 1] = 8.0 * near - 2.0
@@ -428,9 +429,9 @@
     coef = total_of(full_ref, a_ref, b_ref, c_ref)
     for x in range(SLAB):
         taken = dot(coef, core_ref[x])
-        ahead = ahead_ref[x] - taken[: ahead_ref.shape[1]]
-        rest = rest_ref[x] - taken[ahead_ref.shape[1] :]
-        own[x * BATCH : (x + 1) * BATCH] = ahead[:BATCH]
+        ahead = ahead_ref[x] - taken[:BATCH]
+        rest = rest_ref[x] - taken[BATCH:]
+        own[x * BATCH : (x + 1) * BATCH] = ahead
         weighted = jnp.sum(mapped_ref[x].astype(F32) * ahead, axis=0, keepdims=True)
         weighted += jnp.sum(mapped_rest_ref[x].astype(F32) * rest, axis=0, keepdims=True)
         rows[x : x + 1] = weighted / (3.0 * BATCH)
@@ -470,15 +471,15 @@
 
     mate, line.token = lax.optimization_barrier((mate, line.token))
     second = permute_groups(mate, [(i, (i + 2) % groups) for i in range(0, groups, 2)])
-    mapped, full, half = map_batches(line, pick, core_x, [(stochastic,), (third,)])
+    mapped, full, half = map_batches(line, pick, core_x, [(stochastic,)])
     others = exchange(half)
     field, low, high = project(line, full, others, mapped, core_x, local)
     below = lax.ppermute(high, "grid", UP)
     above = lax.ppermute(low, "grid", DOWN)
 
-    mapped_rest, full, half = map_batches(line, pick, core_x, [(mate, second)])
-    others = exchange(half)
-    rest, low, high = project(line, full, others, mapped_rest, core_x, None)
+    batches = [(third,), (mate, second)]
+    mapped_rest, full, half = map_batches(line, pick, core_x, batches)
+    rest, low, high = project(line, full, exchange(half), mapped_rest, core_x, None)
     below_rest, above_rest = lax.ppermute(high, "grid", UP), lax.ppermute(low, "grid", DOWN)
 
     weight, ahead = filter_ahead(line, field, below, above, local)

time: 102 us -> 89.5 us (0.88); the launches traced: 101 us -> 89.3 us
  waiting for transfers between devices: 34.3 us -> 14.2 us
  starting transfers between devices: 22.4 us -> 31.9 us
    ppermute x3, waiting for transfers between devices: 24.4 us -> 7.6 us  [permute_groups(): return lax.ppermute(array, 'group', pairs)]
    ppermute x9, starting transfers between devices: 7.98 us -> 14 us  [exchange(): lax.ppermute(half, 'grid', [(i, i ^ k) for i in range(GRID)])]
    ppermute x9, waiting for transfers between devices: 9.89 us -> 6.6 us  [exchange(): lax.ppermute(half, 'grid', [(i, i ^ k) for i in range(GRID)])]
    ppermute x3, starting transfers between devices: 7.22 us -> 9.16 us  [permute_groups(): return lax.ppermute(array, 'group', pairs)]
    ppermute x1, starting transfers between devices: 2.49 us -> 3.75 us  [body(): lax.ppermute(high, 'grid', UP)]
  transfers between devices with their start and end apart: 16 -> 16, of which waited for: 9 -> 6; matrix products, arithmetic and copies ran while one was open for 0% -> 0% of each run, Pallas kernels for 25% -> 23%
where the time goes in v3:
time: 89.5 us; the launch traced here: 89.3 us
  Pallas kernels  42.4 us (47%)
  starting transfers between devices  31.9 us (36%)
  waiting for transfers between devices  14.2 us (16%)
    pallas_call x9, Pallas kernels, call(): pl.pallas_call(with_token, in_specs=specs, out_specs=tuple((VMEM for _ in...  42.4 us
    ppermute x9, starting transfers between devices, exchange(): lax.ppermute(half, 'grid', [(i, i ^ k) for i in range(GRID)])  14 us
    ppermute x3, starting transfers between devices, permute_groups(): return lax.ppermute(array, 'group', pairs)  9.16 us
    ppermute x3, waiting for transfers between devices, permute_groups(): return lax.ppermute(array, 'group', pairs)  7.6 us
    ppermute x9, waiting for transfers between devices, exchange(): lax.ppermute(half, 'grid', [(i, i ^ k) for i in range(GRID)])  6.6 us
    ppermute x1, starting transfers between devices, body(): lax.ppermute(high, 'grid', UP)  3.75 us
    ppermute x1, starting transfers between devices, body(): below = lax.ppermute(high, 'grid', UP)  2.23 us
  transfers between devices with their start and end apart: 16, of which 6 were waited for; matrix products, arithmetic and copies ran while one was open for 0% of the time, Pallas kernels for 23%

profile of v3, /device:TPU:0, one launch (start us, length us, event | category | flops | bytes accessed | tf_op | source)
XLA Modules:
  0.0 89.3 jit_solution(4595561969958415718)
XLA Ops:
  0.6 3.4 %collective-permute-start.1 = (bf16[32,8,1024]{2,1,0:T(8,128)(2,1)}, bf16[32,8,1024]{2,1,0:T(8,128)(2,1)S(1)}, u32[]{:S(2)}, u32[]{:S(2)}) collective-permute-start(bf16[32,8,1024]{2,1,0:T(8,128)(2,1)} %param.4), channel_id=1, source_target_pairs={{0,4},{4,0},{8,12},{12,8},{16,20},{20,16},{24,28},{28,24},{32,36},... | collective-permute-start | bytes 1572872 | tf_op jit(solution)/shard_map/ppermute | solution.py:460
  4.0 1.9 %collective-permute-start = (bf16[32,8,1024]{2,1,0:T(8,128)(2,1)}, bf16[32,8,1024]{2,1,0:T(8,128)(2,1)S(1)}, u32[]{:S(2)}, u32[]{:S(2)}) collective-permute-start(bf16[32,8,1024]{2,1,0:T(8,128)(2,1)} %param.4), channel_id=1, source_target_pairs={{0,8},{4,12},{8,16},{12,20},{16,24},{20,28},{24,32},{28,36},{32,40... | collective-permute-start | bytes 1572872 | tf_op jit(solution)/shard_map/ppermute | solution.py:460
  5.9 0.0 copy-start.1
  5.9 0.0 copy-start.2
  5.9 7.2 %shard_map.59 = (bf16[8,512,1024]{2,1,0:T(8,128)(2,1)S(1)}, f32[8,128]{1,0:T(8,128)S(1)}) custom-call(bf16[4096,1024]{1,0:T(8,128)(2,1)} %bitcast.13), custom_call_target="tpu_custom_call" | custom-call | flops 4000000000 | bytes 1024 | tf_op jit(solution)/shard_map/pallas_call | solution.py:74
  13.1 0.0 copy-start
  13.2 0.0 copy-done.1
  13.2 0.0 copy-done.2
  13.2 1.8 %shard_map.60 = (bf16[1024,1024]{1,0:T(8,128)(2,1)S(1)}, bf16[1024,1024]{1,0:T(8,128)(2,1)S(1)}, f32[8,1024]{1,0:T(8,128)S(1)}, f32[8,128]{1,0:T(8,128)S(1)}) custom-call(s32[1,1024]{1,0:T(1,128)S(1)} %copy-done.2, f32[8,1024]{1,0:T(8,128)S(1)} %bitcast.12, f32[8,128]{1,0:T(8,128)S(1)} %get-tuple-element.37.refs_2_), custom_call_target="tpu_custom_call" | custom-call | flops 1000000000 | bytes 1024 | tf_op jit(solution)/shard_map/pallas_call | solution.py:74
  15.0 1.1 %collective-permute-done.1 = bf16[32,8,1024]{2,1,0:T(8,128)(2,1)S(1)} collective-permute-done((bf16[32,8,1024]{2,1,0:T(8,128)(2,1)}, bf16[32,8,1024]{2,1,0:T(8,128)(2,1)S(1)}, u32[]{:S(2)}, u32[]{:S(2)}) %collective-permute-start.1) | collective-permute-done | bytes 524320 | tf_op jit(solution)/shard_map/ppermute | solution.py:460
  16.2 3.9 %collective-permute-start.2 = (bf16[32,8,1024]{2,1,0:T(8,128)(2,1)S(1)}, bf16[32,8,1024]{2,1,0:T(8,128)(2,1)S(1)}, u32[]{:S(2)}, u32[]{:S(2)}) collective-permute-start(bf16[32,8,1024]{2,1,0:T(8,128)(2,1)S(1)} %collective-permute-done.1), channel_id=1, source_target_pairs={{0,8},{8,16},{16,24},{24,32},{32,40},{40,48},{48,56},{56,64},{64,7... | collective-permute-start | bytes 1572872 | tf_op jit(solution)/shard_map/ppermute | solution.py:460
  20.0 0.0 copy-done
  20.0 3.2 %shard_map.61 = (bf16[8,32,1024]{2,1,0:T(8,128)(2,1)S(1)}, f32[32,512]{1,0:T(8,128)S(1)}, bf16[32,512]{1,0:T(8,128)(2,1)S(1)}, f32[8,128]{1,0:T(8,128)S(1)}) custom-call(bf16[1024,1024]{1,0:T(8,128)(2,1)S(1)} %get-tuple-element.38.refs_0_, bf16[8,512,1024]{2,1,0:T(8,128)(2,1)S(1)} %get-tuple-element.39.refs_1_.refs_5_.refs_6_.refs_8_, ...), custom_call_target="tpu_custom_call" | custom-call | flops 1000000000 | bytes 1024 | tf_op jit(solution)/shard_map/pallas_call | solution.py:74
  23.3 0.0 collective-permute-start.5
  23.3 1.7 %collective-permute-start.4 = (bf16[32,512]{1,0:T(8,128)(2,1)S(1)}, bf16[32,512]{1,0:T(8,128)(2,1)S(1)}, u32[]{:S(2)}, u32[]{:S(2)}) collective-permute-start(bf16[32,512]{1,0:T(8,128)(2,1)S(1)} %get-tuple-element.44), channel_id=1, source_target_pairs={{0,2},{1,3},{2,0},{3,1},{4,6},{5,7},{6,4},{7,5},{8,10},{9,11},{10,... | collective-permute-start | bytes 98312 | tf_op jit(solution)/shard_map/ppermute | solution.py:251
  25.0 0.2 collective-permute-start.3
  25.2 1.7 %collective-permute-done.5.refs_3_ = bf16[32,512]{1,0:T(8,128)(2,1)S(1)} collective-permute-done((bf16[32,512]{1,0:T(8,128)(2,1)S(1)}, bf16[32,512]{1,0:T(8,128)(2,1)S(1)}, u32[]{:S(2)}, u32[]{:S(2)}) %collective-permute-start.5) | collective-permute-done | bytes 32800 | tf_op jit(solution)/shard_map/ppermute | solution.py:251
  26.9 0.5 collective-permute-done.4.refs_2_
  27.4 0.0 collective-permute-done.3.refs_1_
  27.4 1.6 %shard_map.62 = (f32[8,32,1024]{2,1,0:T(8,128)S(1)}, bf16[6,40,1024]{2,1,0:T(8,128)(2,1)S(1)}, bf16[6,40,1024]{2,1,0:T(8,128)(2,1)S(1)}, f32[8,128]{1,0:T(8,128)S(1)}) custom-call(f32[32,512]{1,0:T(8,128)S(1)} %get-tuple-element.43.refs_0_, bf16[32,512]{1,0:T(8,128)(2,1)S(1)} %collective-permute-done.3.refs_1_, ...), custom_call_target="tpu_custom_call" | custom-call | flops 1000000000 | bytes 1024 | tf_op jit(solution)/shard_map/pallas_call | solution.py:74
  28.9 0.0 collective-permute-done
  28.9 6.4 %collective-permute-done.2 = bf16[32,8,1024]{2,1,0:T(8,128)(2,1)S(1)} collective-permute-done((bf16[32,8,1024]{2,1,0:T(8,128)(2,1)S(1)}, bf16[32,8,1024]{2,1,0:T(8,128)(2,1)S(1)}, u32[]{:S(2)}, u32[]{:S(2)}) %collective-permute-start.2) | collective-permute-done | bytes 524320 | tf_op jit(solution)/shard_map/ppermute | solution.py:460
  35.4 4.1 %shard_map.63 = (bf16[8,64,1024]{2,1,0:T(8,128)(2,1)S(1)}, f32[64,512]{1,0:T(8,128)S(1)}, bf16[64,512]{1,0:T(8,128)(2,1)S(1)}, f32[8,128]{1,0:T(8,128)S(1)}) custom-call(bf16[1024,1024]{1,0:T(8,128)(2,1)S(1)} %get-tuple-element.38.refs_0_, bf16[8,512,1024]{2,1,0:T(8,128)(2,1)S(1)} %get-tuple-element.39.refs_1_.refs_5_.refs_6_.refs_8_, ...), custom_call_target="tpu_custom_call" | custom-call | flops 1500000000 | bytes 1024 | tf_op jit(solution)/shard_map/pallas_call | solution.py:74
  39.5 0.1 collective-permute-start.8
  39.5 1.6 %collective-permute-start.7 = (bf16[64,512]{1,0:T(8,128)(2,1)S(1)}, bf16[64,512]{1,0:T(8,128)(2,1)S(1)}, u32[]{:S(2)}, u32[]{:S(2)}) collective-permute-start(bf16[64,512]{1,0:T(8,128)(2,1)S(1)} %get-tuple-element.50), channel_id=1, source_target_pairs={{0,2},{1,3},{2,0},{3,1},{4,6},{5,7},{6,4},{7,5},{8,10},{9,11},{10,... | collective-permute-start | bytes 196616 | tf_op jit(solution)/shard_map/ppermute | solution.py:251
  41.2 0.2 collective-permute-start.6
  41.4 2.2 %collective-permute-start.11 = (bf16[6,40,1024]{2,1,0:T(8,128)(2,1)S(1)}, bf16[6,40,1024]{2,1,0:T(8,128)(2,1)S(1)}, u32[]{:S(2)}, u32[]{:S(2)}) collective-permute-start(bf16[6,40,1024]{2,1,0:T(8,128)(2,1)S(1)} %get-tuple-element.57), channel_id=1, source_target_pairs={{0,1},{1,2},{2,3},{4,5},{5,6},{6,7},{8,9},{9,10},{10,11},{12,13},{... | collective-permute-start | bytes 1474568 | tf_op jit(solution)/shard_map/ppermute | solution.py:477
  43.6 1.5 %collective-permute-start.12 = (bf16[6,40,1024]{2,1,0:T(8,128)(2,1)S(1)}, bf16[6,40,1024]{2,1,0:T(8,128)(2,1)S(1)}, u32[]{:S(2)}, u32[]{:S(2)}) collective-permute-start(bf16[6,40,1024]{2,1,0:T(8,128)(2,1)S(1)} %get-tuple-element.58), channel_id=1, source_target_pairs={{1,0},{2,1},{3,2},{5,4},{6,5},{7,6},{9,8},{10,9},{11,10},{13,12},{... | collective-permute-start | bytes 1474568 | tf_op jit(solution)/shard_map/ppermute | solution.py:478
  45.1 0.0 collective-permute-done.8.refs_3_
  45.1 0.2 collective-permute-done.7.refs_2_
  45.3 0.0 collective-permute-done.6.refs_1_
  45.3 1.6 %shard_map.64 = (f32[8,64,1024]{2,1,0:T(8,128)S(1)}, bf16[6,64,1024]{2,1,0:T(8,128)(2,1)S(1)}, bf16[6,64,1024]{2,1,0:T(8,128)(2,1)S(1)}, f32[8,128]{1,0:T(8,128)S(1)}) custom-call(f32[64,512]{1,0:T(8,128)S(1)} %get-tuple-element.49.refs_0_, bf16[64,512]{1,0:T(8,128)(2,1)S(1)} %collective-permute-done.6.refs_1_, ...), custom_call_target="tpu_custom_call" | custom-call | flops 1000000000 | bytes 1024 | tf_op jit(solution)/shard_map/pallas_call | solution.py:74
  46.9 3.7 %collective-permute-start.9 = (bf16[6,64,1024]{2,1,0:T(8,128)(2,1)S(1)}, bf16[6,64,1024]{2,1,0:T(8,128)(2,1)S(1)}, u32[]{:S(2)}, u32[]{:S(2)}) collective-permute-start(bf16[6,64,1024]{2,1,0:T(8,128)(2,1)S(1)} %get-tuple-element.54), channel_id=1, source_target_pairs={{0,1},{1,2},{2,3},{4,5},{5,6},{6,7},{8,9},{9,10},{10,11},{12,13},{... | collective-permute-start | bytes 2359304 | tf_op jit(solution)/shard_map/ppermute | solution.py:483
  50.7 1.3 %collective-permute-start.10 = (bf16[6,64,1024]{2,1,0:T(8,128)(2,1)S(1)}, bf16[6,64,1024]{2,1,0:T(8,128)(2,1)S(1)}, u32[]{:S(2)}, u32[]{:S(2)}) collective-permute-start(bf16[6,64,1024]{2,1,0:T(8,128)(2,1)S(1)} %get-tuple-element.55), channel_id=1, source_target_pairs={{1,0},{2,1},{3,2},{5,4},{6,5},{7,6},{9,8},{10,9},{11,10},{13,12},{... | collective-permute-start | bytes 2359304 | tf_op jit(solution)/shard_map/ppermute | solution.py:483
  52.0 0.0 collective-permute-done.11.refs_1_
  52.0 0.0 collective-permute-done.12.refs_2_
  52.0 5.2 %shard_map.65 = (f32[20,1024]{1,0:T(8,128)S(1)}, f32[20,1024]{1,0:T(8,128)S(1)}, f32[2,8,128]{2,1,0:T(8,128)S(1)}, f32[8,32,1024]{2,1,0:T(8,128)S(1)}, f32[8,128]{1,0:T(8,128)S(1)}) custom-call(f32[8,32,1024]{2,1,0:T(8,128)S(1)} %get-tuple-element.56.refs_0_, bf16[6,40,1024]{2,1,0:T(8,128)(2,1)S(1)} %collective-permute-done.11.refs_1_, ...), custom_call_target="tpu_custom_call" | custom-call | flops 3500000000 | bytes 1024 | tf_op jit(solution)/shard_map/pallas_call | solution.py:74
  57.2 0.0 collective-permute-done.9.refs_1_
  57.2 0.0 collective-permute-done.10.refs_2_
  57.2 13.4 %shard_map.66 = (f32[8,64,1024]{2,1,0:T(8,128)S(1)}, f32[96,512]{1,0:T(8,128)S(1)}, bf16[96,512]{1,0:T(8,128)(2,1)S(1)}, f32[8,128]{1,0:T(8,128)S(1)}) custom-call(f32[8,64,1024]{2,1,0:T(8,128)S(1)} %get-tuple-element.53.refs_0_, bf16[6,64,1024]{2,1,0:T(8,128)(2,1)S(1)} %collective-permute-done.9.refs_1_, ...), custom_call_target="tpu_custom_call" | custom-call | flops 7000000000 | bytes 1024 | tf_op jit(solution)/shard_map/pallas_call | solution.py:74
  70.7 2.4 %collective-permute-start.15 = (bf16[96,512]{1,0:T(8,128)(2,1)S(1)}, bf16[96,512]{1,0:T(8,128)(2,1)S(1)}, u32[]{:S(2)}, u32[]{:S(2)}) collective-permute-start(bf16[96,512]{1,0:T(8,128)(2,1)S(1)} %get-tuple-element.66), channel_id=1, source_target_pairs={{0,3},{1,2},{2,1},{3,0},{4,7},{5,6},{6,5},{7,4},{8,11},{9,10},{10,... | collective-permute-start | bytes 294920 | tf_op jit(solution)/shard_map/ppermute | solution.py:251
  73.1 7.7 %collective-permute-start.14 = (bf16[96,512]{1,0:T(8,128)(2,1)S(1)}, bf16[96,512]{1,0:T(8,128)(2,1)S(1)}, u32[]{:S(2)}, u32[]{:S(2)}) collective-permute-start(bf16[96,512]{1,0:T(8,128)(2,1)S(1)} %get-tuple-element.66), channel_id=1, source_target_pairs={{0,2},{1,3},{2,0},{3,1},{4,6},{5,7},{6,4},{7,5},{8,10},{9,11},{10,... | collective-permute-start | bytes 294920 | tf_op jit(solution)/shard_map/ppermute | solution.py:251
  80.8 0.0 collective-permute-start.13
  80.8 0.0 collective-permute-done.15.refs_3_
  80.8 4.2 %collective-permute-done.14.refs_2_ = bf16[96,512]{1,0:T(8,128)(2,1)S(1)} collective-permute-done((bf16[96,512]{1,0:T(8,128)(2,1)S(1)}, bf16[96,512]{1,0:T(8,128)(2,1)S(1)}, u32[]{:S(2)}, u32[]{:S(2)}) %collective-permute-start.14) | collective-permute-done | bytes 98336 | tf_op jit(solution)/shard_map/ppermute | solution.py:251
  85.0 0.0 collective-permute-done.13.refs_1_
  85.1 4.3 %shard_map.67 = (f32[256,1024]{1,0:T(8,128)}, f32[8,1024]{1,0:T(8,128)}, f32[8,128]{1,0:T(8,128)}) custom-call(f32[96,512]{1,0:T(8,128)S(1)} %get-tuple-element.65.refs_0_, bf16[96,512]{1,0:T(8,128)(2,1)S(1)} %collective-permute-done.13.refs_1_, bf16[96,512]{1,0:T(8,128)(2,1)S(1)} %collective-permute-done.14.refs_2_, ...), custom_call_target="tpu_custom_call" | custom-call | flops 2000000000 | bytes 1024 | tf_op jit(solution)/shard_map/pallas_call | solution.py:74
Async XLA Ops:
  0.6 15.5 %collective-permute-start.1 = (bf16[32,8,1024]{2,1,0:T(8,128)(2,1)}, bf16[32,8,1024]{2,1,0:T(8,128)(2,1)S(1)}, u32[]{:S(2)}, u32[]{:S(2)}) collective-permute-start(bf16[32,8,1024]{2,1,0:T(8,128)(2,1)} %param.4), channel_id=1, source_target_pairs={{0,4},{4,0},{8,12},{12,8},{16,20},{20,16},{24,28},{28,24},{32,36},... | collective-permute-start | bytes 1572872 | tf_op jit(solution)/shard_map/ppermute | solution.py:460
  4.0 24.9 %collective-permute-start = (bf16[32,8,1024]{2,1,0:T(8,128)(2,1)}, bf16[32,8,1024]{2,1,0:T(8,128)(2,1)S(1)}, u32[]{:S(2)}, u32[]{:S(2)}) collective-permute-start(bf16[32,8,1024]{2,1,0:T(8,128)(2,1)} %param.4), channel_id=1, source_target_pairs={{0,8},{4,12},{8,16},{12,20},{16,24},{20,28},{24,32},{28,36},{32,40... | collective-permute-start | bytes 1572872 | tf_op jit(solution)/shard_map/ppermute | solution.py:460
  5.9 7.2 %copy-start.1 = (f32[1,8,1024]{2,1,0:T(8,128)S(1)}, f32[1,8,1024]{2,1,0:T(8,128)}, u32[]{:S(2)}) copy-start(f32[1,8,1024]{2,1,0:T(8,128)} %param.7) | copy-start | bytes 98308
  5.9 7.2 %copy-start.2 = (s32[1,1024]{1,0:T(1,128)S(1)}, s32[1,1024]{1,0:T(1,128)}, u32[]{:S(2)}) copy-start(s32[1,1024]{1,0:T(1,128)} %refs_0_.1) | copy-start | bytes 12292
  13.1 6.9 %copy-start = (bf16[32,8,1024]{2,1,0:T(8,128)(2,1)S(1)}, bf16[32,8,1024]{2,1,0:T(8,128)(2,1)}, u32[]{:S(2)}) copy-start(bf16[32,8,1024]{2,1,0:T(8,128)(2,1)} %param.4) | copy-start | bytes 1572868
  16.2 19.2 %collective-permute-start.2 = (bf16[32,8,1024]{2,1,0:T(8,128)(2,1)S(1)}, bf16[32,8,1024]{2,1,0:T(8,128)(2,1)S(1)}, u32[]{:S(2)}, u32[]{:S(2)}) collective-permute-start(bf16[32,8,1024]{2,1,0:T(8,128)(2,1)S(1)} %collective-permute-done.1), channel_id=1, source_target_pairs={{0,8},{8,16},{16,24},{24,32},{32,40},{40,48},{48,56},{56,64},{64,7... | collective-permute-start | bytes 1572872 | tf_op jit(solution)/shard_map/ppermute | solution.py:460
  23.3 3.6 %collective-permute-start.5 = (bf16[32,512]{1,0:T(8,128)(2,1)S(1)}, bf16[32,512]{1,0:T(8,128)(2,1)S(1)}, u32[]{:S(2)}, u32[]{:S(2)}) collective-permute-start(bf16[32,512]{1,0:T(8,128)(2,1)S(1)} %get-tuple-element.44), channel_id=1, source_target_pairs={{0,3},{1,2},{2,1},{3,0},{4,7},{5,6},{6,5},{7,4},{8,11},{9,10},{10,... | collective-permute-start | bytes 98312 | tf_op jit(solution)/shard_map/ppermute | solution.py:251
  23.3 4.0 %collective-permute-start.4 = (bf16[32,512]{1,0:T(8,128)(2,1)S(1)}, bf16[32,512]{1,0:T(8,128)(2,1)S(1)}, u32[]{:S(2)}, u32[]{:S(2)}) collective-permute-start(bf16[32,512]{1,0:T(8,128)(2,1)S(1)} %get-tuple-element.44), channel_id=1, source_target_pairs={{0,2},{1,3},{2,0},{3,1},{4,6},{5,7},{6,4},{7,5},{8,10},{9,11},{10,... | collective-permute-start | bytes 98312 | tf_op jit(solution)/shard_map/ppermute | solution.py:251
  25.0 2.4 %collective-permute-start.3 = (bf16[32,512]{1,0:T(8,128)(2,1)S(1)}, bf16[32,512]{1,0:T(8,128)(2,1)S(1)}, u32[]{:S(2)}, u32[]{:S(2)}) collective-permute-start(bf16[32,512]{1,0:T(8,128)(2,1)S(1)} %get-tuple-element.44), channel_id=1, source_target_pairs={{0,1},{1,0},{2,3},{3,2},{4,5},{5,4},{6,7},{7,6},{8,9},{9,8},{10,11... | collective-permute-start | bytes 98312 | tf_op jit(solution)/shard_map/ppermute | solution.py:251
  39.5 5.7 %collective-permute-start.8 = (bf16[64,512]{1,0:T(8,128)(2,1)S(1)}, bf16[64,512]{1,0:T(8,128)(2,1)S(1)}, u32[]{:S(2)}, u32[]{:S(2)}) collective-permute-start(bf16[64,512]{1,0:T(8,128)(2,1)S(1)} %get-tuple-element.50), channel_id=1, source_target_pairs={{0,3},{1,2},{2,1},{3,0},{4,7},{5,6},{6,5},{7,4},{8,11},{9,10},{10,... | collective-permute-start | bytes 196616 | tf_op jit(solution)/shard_map/ppermute | solution.py:251
  39.5 5.8 %collective-permute-start.7 = (bf16[64,512]{1,0:T(8,128)(2,1)S(1)}, bf16[64,512]{1,0:T(8,128)(2,1)S(1)}, u32[]{:S(2)}, u32[]{:S(2)}) collective-permute-start(bf16[64,512]{1,0:T(8,128)(2,1)S(1)} %get-tuple-element.50), channel_id=1, source_target_pairs={{0,2},{1,3},{2,0},{3,1},{4,6},{5,7},{6,4},{7,5},{8,10},{9,11},{10,... | collective-permute-start | bytes 196616 | tf_op jit(solution)/shard_map/ppermute | solution.py:251
  41.2 4.1 %collective-permute-start.6 = (bf16[64,512]{1,0:T(8,128)(2,1)S(1)}, bf16[64,512]{1,0:T(8,128)(2,1)S(1)}, u32[]{:S(2)}, u32[]{:S(2)}) collective-permute-start(bf16[64,512]{1,0:T(8,128)(2,1)S(1)} %get-tuple-element.50), channel_id=1, source_target_pairs={{0,1},{1,0},{2,3},{3,2},{4,5},{5,4},{6,7},{7,6},{8,9},{9,8},{10,11... | collective-permute-start | bytes 196616 | tf_op jit(solution)/shard_map/ppermute | solution.py:251
  41.4 10.6 %collective-permute-start.11 = (bf16[6,40,1024]{2,1,0:T(8,128)(2,1)S(1)}, bf16[6,40,1024]{2,1,0:T(8,128)(2,1)S(1)}, u32[]{:S(2)}, u32[]{:S(2)}) collective-permute-start(bf16[6,40,1024]{2,1,0:T(8,128)(2,1)S(1)} %get-tuple-element.57), channel_id=1, source_target_pairs={{0,1},{1,2},{2,3},{4,5},{5,6},{6,7},{8,9},{9,10},{10,11},{12,13},{... | collective-permute-start | bytes 1474568 | tf_op jit(solution)/shard_map/ppermute | solution.py:477
  43.6 8.3 %collective-permute-start.12 = (bf16[6,40,1024]{2,1,0:T(8,128)(2,1)S(1)}, bf16[6,40,1024]{2,1,0:T(8,128)(2,1)S(1)}, u32[]{:S(2)}, u32[]{:S(2)}) collective-permute-start(bf16[6,40,1024]{2,1,0:T(8,128)(2,1)S(1)} %get-tuple-element.58), channel_id=1, source_target_pairs={{1,0},{2,1},{3,2},{5,4},{6,5},{7,6},{9,8},{10,9},{11,10},{13,12},{... | collective-permute-start | bytes 1474568 | tf_op jit(solution)/shard_map/ppermute | solution.py:478
  46.9 10.3 %collective-permute-start.9 = (bf16[6,64,1024]{2,1,0:T(8,128)(2,1)S(1)}, bf16[6,64,1024]{2,1,0:T(8,128)(2,1)S(1)}, u32[]{:S(2)}, u32[]{:S(2)}) collective-permute-start(bf16[6,64,1024]{2,1,0:T(8,128)(2,1)S(1)} %get-tuple-element.54), channel_id=1, source_target_pairs={{0,1},{1,2},{2,3},{4,5},{5,6},{6,7},{8,9},{9,10},{10,11},{12,13},{... | collective-permute-start | bytes 2359304 | tf_op jit(solution)/shard_map/ppermute | solution.py:483
  50.7 6.6 %collective-permute-start.10 = (bf16[6,64,1024]{2,1,0:T(8,128)(2,1)S(1)}, bf16[6,64,1024]{2,1,0:T(8,128)(2,1)S(1)}, u32[]{:S(2)}, u32[]{:S(2)}) collective-permute-start(bf16[6,64,1024]{2,1,0:T(8,128)(2,1)S(1)} %get-tuple-element.55), channel_id=1, source_target_pairs={{1,0},{2,1},{3,2},{5,4},{6,5},{7,6},{9,8},{10,9},{11,10},{13,12},{... | collective-permute-start | bytes 2359304 | tf_op jit(solution)/shard_map/ppermute | solution.py:483
  70.7 10.2 %collective-permute-start.15 = (bf16[96,512]{1,0:T(8,128)(2,1)S(1)}, bf16[96,512]{1,0:T(8,128)(2,1)S(1)}, u32[]{:S(2)}, u32[]{:S(2)}) collective-permute-start(bf16[96,512]{1,0:T(8,128)(2,1)S(1)} %get-tuple-element.66), channel_id=1, source_target_pairs={{0,3},{1,2},{2,1},{3,0},{4,7},{5,6},{6,5},{7,4},{8,11},{9,10},{10,... | collective-permute-start | bytes 294920 | tf_op jit(solution)/shard_map/ppermute | solution.py:251
  73.1 11.9 %collective-permute-start.14 = (bf16[96,512]{1,0:T(8,128)(2,1)S(1)}, bf16[96,512]{1,0:T(8,128)(2,1)S(1)}, u32[]{:S(2)}, u32[]{:S(2)}) collective-permute-start(bf16[96,512]{1,0:T(8,128)(2,1)S(1)} %get-tuple-element.66), channel_id=1, source_target_pairs={{0,2},{1,3},{2,0},{3,1},{4,6},{5,7},{6,4},{7,5},{8,10},{9,11},{10,... | collective-permute-start | bytes 294920 | tf_op jit(solution)/shard_map/ppermute | solution.py:251
  80.8 4.2 %collective-permute-start.13 = (bf16[96,512]{1,0:T(8,128)(2,1)S(1)}, bf16[96,512]{1,0:T(8,128)(2,1)S(1)}, u32[]{:S(2)}, u32[]{:S(2)}) collective-permute-start(bf16[96,512]{1,0:T(8,128)(2,1)S(1)} %get-tuple-element.66), channel_id=1, source_target_pairs={{0,1},{1,0},{2,3},{3,2},{4,5},{5,4},{6,7},{7,6},{8,9},{9,8},{10,11... | collective-permute-start | bytes 294920 | tf_op jit(solution)/shard_map/ppermute | solution.py:251
